TPU v7x, 128 devices: a whole 4x4x4 slice. The times are simulated.
128 devices in a mesh: req: 16 (over z, x), kv: 8 (over y, core).
Axes of the slice: x: 4, y: 4, z: 4, core: 2. Of those that a mesh axis runs over, the one named last changes fastest.
Arguments:
- hidden_in: bfloat16 [2048, 1536], P('req'), may hold values from -6 to 6
- attn_gain: float32 [1536], replicated, may hold values from 0.1 to 1.9
- w_query: bfloat16 [1536, 1536], P('kv'), may hold values from -0.15625 to 0.15625
- w_key: bfloat16 [512, 1536], P('kv'), may hold values from -0.15625 to 0.15625
- w_value: bfloat16 [512, 1536], P('kv'), may hold values from -0.15625 to 0.15625
- w_out: bfloat16 [1536, 1536], P('kv'), may hold values from -0.75 to 0.75
- k_cache: bfloat16 [6144, 8, 8192], P('req', 'kv'), may hold values from -600 to 600
- v_cache: bfloat16 [6144, 8, 8192], P('req', 'kv'), may hold values from -6 to 6
- cache_len: int32 [2048], replicated, may hold values from 1 to 384, 393216 in all
- block_slot: int32 [6144], P('req'), may hold values from 0 to 6143, as said below
- moe_gain: float32 [1536], replicated, may hold values from 0.1 to 1.9
- w_router: bfloat16 [1536, 32], replicated, may hold values from -0.15625 to 0.15625
- w_gate_up: bfloat16 [32, 1536, 1024], P('req'), may hold values from -0.15625 to 0.15625
- w_down: bfloat16 [32, 512, 1536], P('req'), may hold values from -0.25 to 0.25
- routes: int32 [2048, 8], P(('req', 'kv')), may hold values from 0 to 31, all different within a row; in each aligned block of 16 rows (0 to 15, 16 to 31, ...) at most 16 rows name the same one
Outputs:
- layer_out: bfloat16 [2048, 1536], P(('req', 'kv'))
Inputs may be any that keep to these rules, and one draw needn't show every extreme that they name: `block_slot`: each value once; the block holds page v % 3 of request v // 3; the blocks of one index of req hold exactly 128 * 3 / 16 pages of the requests of each index of req. `routes`: each row names 8 different experts; in the 16 rows of one device an expert may be named by all of them.
All inputs are finite; a program needn't handle non-finite values.
Results may differ from a plain program's by a relative error of at most 0.02.
The roundings to bfloat16 on the way count: a program that leaves them out, or rounds other values in their place, can miss the bound.
Values may be sent and summed in bfloat16 or wider, within the bound.
A program may use at most 192 MiB of HBM per device.

v0:
```python
import jax
import jax.numpy as jnp
from jax import lax
from jax.sharding import PartitionSpec as P

HD = 64
FFE = 512
BLK = 128
PAGES = 3


def merged_2(value, axis, join):
    pieces = jax.tree.map(lambda part: lax.all_gather(part, axis), value)
    head = jax.tree.map(lambda part: part[0], pieces)
    tail = jax.tree.map(lambda part: part[1:], pieces)
    so_far, _ = lax.scan(lambda so_far, share: (join(so_far, share), None), head, tail)
    return so_far


def rms_norm(values, gain):
    values = values.astype(jnp.float32)
    return values * lax.rsqrt(jnp.mean(values * values, -1, keepdims=True) + 1e-05) * gain


def rotate(values, positions):
    half_dim = values.shape[-1] // 2
    frequency = 10000.0 ** (-jnp.arange(half_dim, dtype=jnp.float32) / half_dim)
    angles = positions.astype(jnp.float32)[:, None, None] * frequency
    cosines = jnp.cos(angles)
    sines = jnp.sin(angles)
    first_half = values[..., :half_dim]
    second_half = values[..., half_dim:]
    return jnp.concatenate(
        [first_half * cosines - second_half * sines, first_half * sines + second_half * cosines], -1
    )


def project_rows(normed, weight):
    return lax.dot_general(
        normed, weight, (((1,), (1,)), ((), ())), preferred_element_type=jnp.float32
    )


def shards(
    hidden_in,
    attn_gain,
    w_query,
    w_key,
    w_value,
    w_out,
    k_cache,
    v_cache,
    cache_len,
    block_slot,
    moe_gain,
    w_router,
    w_gate_up,
    w_down,
    routes,
):
    req_index = lax.axis_index("req")
    kv_index = lax.axis_index("kv")
    row_count = hidden_in.shape[0]
    heads_dev = w_query.shape[0] // HD
    kv_dev = w_key.shape[0] // HD
    per_group = heads_dev // kv_dev
    block_count = k_cache.shape[0]
    request_count = cache_len.shape[0]
    home_start = req_index * row_count
    lengths_home = lax.dynamic_slice_in_dim(cache_len, home_start, row_count, 0)
    normed = rms_norm(hidden_in, attn_gain).astype(jnp.bfloat16)
    query = project_rows(normed, w_query).reshape(row_count, heads_dev, HD)
    query = (rotate(query, lengths_home) * 0.125).astype(jnp.bfloat16)
    key_new = project_rows(normed, w_key).reshape(row_count, kv_dev, HD)
    key_new = rotate(key_new, lengths_home).astype(jnp.bfloat16)
    value_new = project_rows(normed, w_value).astype(jnp.bfloat16).reshape(row_count, kv_dev, HD)
    queries = lax.all_gather(query.reshape(row_count, heads_dev * HD), "req", axis=0, tiled=True)
    owners = block_slot // PAGES
    pages_of = block_slot % PAGES
    query_blocks = queries[owners].reshape(block_count, kv_dev, per_group, HD)
    cache_keys = k_cache.reshape(block_count, kv_dev, BLK, HD)
    cache_values = v_cache.reshape(block_count, kv_dev, BLK, HD).astype(jnp.float32)
    scores = jnp.einsum(
        "bgqd,bgtd->bgqt", query_blocks, cache_keys, preferred_element_type=jnp.float32
    )
    limits = cache_len[owners]
    usable = pages_of[:, None] * BLK + jnp.arange(BLK, dtype=jnp.int32)[None, :] < limits[:, None]
    usable = usable[:, None, None, :]
    scores = jnp.where(usable, scores, -1e30)
    block_max = jnp.max(scores, -1).reshape(block_count, heads_dev)
    member = owners[None, :] == jnp.arange(request_count, dtype=jnp.int32)[:, None]
    member_float = member.astype(jnp.float32)
    local_max = jnp.max(jnp.where(member[:, :, None], block_max[None, :, :], -1e30), 1)

    def blend_parts(first, second):
        highest = jnp.maximum(first[0], second[0])
        first_scale = jnp.exp(first[0] - highest)
        second_scale = jnp.exp(second[0] - highest)
        first_numer = first[2].reshape(-1, heads_dev, HD) * first_scale[..., None]
        second_numer = second[2].reshape(-1, heads_dev, HD) * second_scale[..., None]
        return (
            highest,
            first[1] * first_scale + second[1] * second_scale,
            (first_numer + second_numer).reshape(-1, heads_dev * HD),
        )

    offsets = local_max[owners].reshape(block_count, kv_dev, per_group)
    weights = jnp.where(usable, jnp.exp(scores - offsets[..., None]), 0.0)
    totals = jnp.sum(weights, -1).reshape(block_count, heads_dev)
    numer = jnp.einsum(
        "bgqt,bgtd->bgqd", weights, cache_values, precision=lax.Precision.HIGHEST
    ).reshape(block_count, heads_dev * HD)
    totals, numer = (totals, numer)
    totals = jnp.dot(member_float, totals, precision=lax.Precision.HIGHEST)
    numer = jnp.dot(member_float, numer, precision=lax.Precision.HIGHEST)
    totals, numer = (totals, numer)
    merged = merged_2((local_max, totals, numer), "req", blend_parts)
    max_home = lax.dynamic_slice_in_dim(merged[0], home_start, row_count, 0)
    totals_home = lax.dynamic_slice_in_dim(merged[1], home_start, row_count, 0)
    numer_home = lax.dynamic_slice_in_dim(merged[2], home_start, row_count, 0)
    own_score = jnp.einsum(
        "rgqd,rgd->rgq",
        query.reshape(row_count, kv_dev, per_group, HD),
        key_new,
        preferred_element_type=jnp.float32,
    ).reshape(row_count, heads_dev)
    highest = jnp.maximum(max_home, own_score)
    old_scale = jnp.exp(max_home - highest)
    new_scale = jnp.exp(own_score - highest)
    total = totals_home * old_scale + new_scale
    spread_value = jnp.broadcast_to(
        value_new.astype(jnp.float32)[:, :, None, :], (row_count, kv_dev, per_group, HD)
    ).reshape(row_count, heads_dev, HD)
    numer_all = (
        numer_home.reshape(row_count, heads_dev, HD) * old_scale[..., None]
        + new_scale[..., None] * spread_value
    )
    attended = (
        (numer_all / total[..., None]).reshape(row_count, heads_dev * HD).astype(jnp.bfloat16)
    )
    projected = jnp.dot(attended, w_out, preferred_element_type=jnp.float32)
    attn_rows = lax.psum_scatter(
        projected.astype(jnp.bfloat16), "kv", scatter_dimension=0, tiled=True
    ).astype(jnp.float32)
    token_count = attn_rows.shape[0]
    rows_home = lax.dynamic_slice_in_dim(hidden_in, kv_index * token_count, token_count, 0)
    after_attn = rows_home.astype(jnp.float32) + attn_rows
    moe_in = rms_norm(after_attn, moe_gain).astype(jnp.bfloat16)
    logits = jnp.dot(moe_in, w_router, preferred_element_type=jnp.float32)
    gate_probs = jax.nn.softmax(jnp.take_along_axis(logits, routes, 1), -1)
    expert_count = w_router.shape[1]
    onehot = (
        routes[:, :, None] == jnp.arange(expert_count, dtype=jnp.int32)[None, None, :]
    ).astype(jnp.float32)
    combine_weight = jnp.sum(gate_probs[:, :, None] * onehot, 1)
    sources = lax.axis_size("req")
    local_experts = w_gate_up.shape[0]
    chosen_mask = jnp.sum(onehot, 1)
    outgoing = (chosen_mask.T[:, :, None] * moe_in[None, :, :].astype(jnp.float32)).astype(
        jnp.bfloat16
    )
    arrived = lax.all_to_all(outgoing, "req", split_axis=0, concat_axis=0, tiled=True)
    count = arrived.shape[1]
    grouped = arrived.reshape(sources, local_experts, count, arrived.shape[2])
    gate_up = jnp.einsum("sexd,edf->sexf", grouped, w_gate_up, preferred_element_type=jnp.float32)
    activated = (jax.nn.silu(gate_up[..., :FFE]) * gate_up[..., FFE:]).astype(jnp.bfloat16)
    produced = jnp.einsum(
        "sexf,efd->sexd", activated, w_down, preferred_element_type=jnp.float32
    ).astype(jnp.bfloat16)
    produced = produced.reshape(sources * local_experts, count, produced.shape[3])
    returned = lax.all_to_all(produced, "req", split_axis=0, concat_axis=0, tiled=True)
    mixture = jnp.einsum(
        "te,etd->td", combine_weight, returned.astype(jnp.float32), precision=lax.Precision.HIGHEST
    )
    return (after_attn + mixture).astype(jnp.bfloat16)


def solution(mesh):
    placed = (
        P("req", None),
        P(),
        P("kv", None),
        P("kv", None),
        P("kv", None),
        P("kv", None),
        P("req", "kv", None),
        P("req", "kv", None),
        P(),
        P("req"),
        P(),
        P(),
        P("req", None, None),
        P("req", None, None),
        P(("req", "kv"), None),
    )
    return jax.shard_map(
        shards, mesh=mesh, in_specs=placed, out_specs=P(("req", "kv"), None), check_vma=False
    )
```

profile of v0, /device:TPU:0, one launch (start us, length us, event | category | flops | bytes accessed | tf_op | source)
XLA Modules:
  0.0 562.3 jit_solution(2169042738235262192)
XLA Ops:
  12.1 28.5 %all_gather.21 = bf16[2048,192]{1,0:T(8,128)(2,1)} all-gather(bf16[128,192]{1,0:T(8,128)(2,1)S(1)} %copy.72), channel_id=1, replica_groups=mesh['req'=16,'kv'=8] {'req'}, dimensions={0}, use_global_device_ids=true | all-gather | bytes 835584 | tf_op jit(solution)/shard_map/all_gather | solution.py:77
  49.3 8.6 %copy.74 = bf16[384,1,8192]{0,2,1:T(8,128)(2,1)} copy(bf16[384,1,8192]{2,0,1:T(8,128)(2,1)} %param.23) | data formatting | bytes 12582912 | tf_op args[6]
  57.9 9.6 %copy.76 = bf16[384,128,64]{1,2,0:T(8,128)(2,1)} copy(bf16[384,128,64]{0,2,1:T(8,128)(2,1)} %bitcast.107) | data formatting | bytes 12582912 | tf_op jit(solution)/shard_map/reshape.6
  81.3 8.7 %copy.79 = bf16[384,1,8192]{0,2,1:T(8,128)(2,1)} copy(bf16[384,1,8192]{2,0,1:T(8,128)(2,1)} %param.24) | data formatting | bytes 12582912 | tf_op args[7]
  90.0 9.6 %copy.80 = bf16[384,128,64]{1,2,0:T(8,128)(2,1)} copy(bf16[384,128,64]{0,2,1:T(8,128)(2,1)} %bitcast.108) | data formatting | bytes 12582912 | tf_op jit(solution)/shard_map/reshape.11
  99.6 12.9 %fusion.31 = f32[384,3,64]{2,1,0:T(4,128)} fusion(bf16[384,128,64]{1,2,0:T(8,128)(2,1)} %copy.80, f32[384,3,128]{2,1,0:T(4,128)} %get-tuple-element.110, f32[384,3]{1,0:T(8,128)S(1)} %gather_fusion.2, pred[384,128]{1,0:T(8,128)(4,1)S(1)} %copy-done.9), kind=kOutput, calls=%fused_computation.46 | convolution fusion | flops 113541120 | bytes 7229952 | tf_op jit(solution)/shard_map/bgqt,bgtd->bgqd/dot_general | solution.py:110
  117.0 24.0 %all-gather = f32[32768,3]{0,1:T(4,128)S(1)} all-gather(f32[2048,3]{0,1:T(4,128)S(1)} %select_reduce_fusion), channel_id=2, replica_groups=mesh['req'=16,'kv'=8] {'req'}, dimensions={0}, use_global_device_ids=true | all-gather | bytes 417792 | tf_op jit(solution)/shard_map/all_gather | solution.py:13
  145.5 22.3 %all-gather.1 = f32[32768,3]{0,1:T(4,128)S(1)} all-gather(f32[2048,3]{0,1:T(4,128)S(1)} %fusion.15), channel_id=3, replica_groups=mesh['req'=16,'kv'=8] {'req'}, dimensions={0}, use_global_device_ids=true | all-gather | bytes 417792 | tf_op jit(solution)/shard_map/all_gather | solution.py:13
  169.0 103.8 %all-gather.5.cloned.1.call-done = f32[32768,192]{0,1:T(8,128)} async-done(((f32[2048,192]{0,1:T(8,128)}), f32[32768,192]{0,1:T(8,128)}) %all-gather.5.cloned.1.call-update) | async-done | bytes 25165840 | tf_op jit(solution)/shard_map/all_gather | solution.py:13
  272.8 16.2 %slice.69 = f32[30720,192]{0,1:T(8,128)} slice(f32[32768,192]{0,1:T(8,128)} %all-gather.5.cloned.1.call-done), slice={[2048:32768], [0:192]} | slice | bytes 47185920 | tf_op jit(solution)/shard_map/slice | solution.py:15
  289.0 22.4 %reshape.366 = f32[15,2048,192]{1,0,2:T(8,128)} reshape(f32[30720,192]{0,1:T(8,128)} %slice.69) | data formatting | bytes 47185920 | tf_op jit(solution)/shard_map/slice | solution.py:15
  314.1 144.0 %while.14 = (s32[]{:T(128)}, f32[2048,3]{0,1:T(4,128)S(1)}, f32[2048,3]{0,1:T(4,128)S(1)}, f32[2048,192]{0,1:T(8,128)}, f32[15,2048,3]{1,2,0:T(4,128)}, /*index=...) while((s32[]{:T(128)}, f32[2048,3]{0,1:T(4,128)S(1)}, f32[2048,3]{0,1:T(4,128)S(1)}, ...), condition=%wide.region_5.6_spmd, body=%wide.region_4.5_spmd.sunk | while | flops 1216514 | bytes 20693148 | solution.py:16
  315.0 6.2 %constant_dynamic-slice_fusion.2 = f32[1,2048,192]{1,0,2:T(1,128)S(1)} fusion(f32[15,2048,192]{1,0,2:T(8,128)} %get-tuple-element.184, s32[]{:T(128)S(6)} %copy.121), kind=kLoop, calls=%fused_computation.14.clone.1 | loop fusion | bytes 3145732 | tf_op jit(solution)/shard_map/while/body/jit(dynamic_index_in_dim)/dynamic_slice | solution.py:16
  324.6 6.2 %constant_dynamic-slice_fusion.2 = f32[1,2048,192]{1,0,2:T(1,128)S(1)} fusion(f32[15,2048,192]{1,0,2:T(8,128)} %get-tuple-element.184, s32[]{:T(128)S(6)} %copy.121), kind=kLoop, calls=%fused_computation.14.clone.1 | loop fusion | bytes 3145732 | tf_op jit(solution)/shard_map/while/body/jit(dynamic_index_in_dim)/dynamic_slice | solution.py:16
  334.3 6.2 %constant_dynamic-slice_fusion.2 = f32[1,2048,192]{1,0,2:T(1,128)S(1)} fusion(f32[15,2048,192]{1,0,2:T(8,128)} %get-tuple-element.184, s32[]{:T(128)S(6)} %copy.121), kind=kLoop, calls=%fused_computation.14.clone.1 | loop fusion | bytes 3145732 | tf_op jit(solution)/shard_map/while/body/jit(dynamic_index_in_dim)/dynamic_slice | solution.py:16
  343.9 6.2 %constant_dynamic-slice_fusion.2 = f32[1,2048,192]{1,0,2:T(1,128)S(1)} fusion(f32[15,2048,192]{1,0,2:T(8,128)} %get-tuple-element.184, s32[]{:T(128)S(6)} %copy.121), kind=kLoop, calls=%fused_computation.14.clone.1 | loop fusion | bytes 3145732 | tf_op jit(solution)/shard_map/while/body/jit(dynamic_index_in_dim)/dynamic_slice | solution.py:16
  353.5 6.2 %constant_dynamic-slice_fusion.2 = f32[1,2048,192]{1,0,2:T(1,128)S(1)} fusion(f32[15,2048,192]{1,0,2:T(8,128)} %get-tuple-element.184, s32[]{:T(128)S(6)} %copy.121), kind=kLoop, calls=%fused_computation.14.clone.1 | loop fusion | bytes 3145732 | tf_op jit(solution)/shard_map/while/body/jit(dynamic_index_in_dim)/dynamic_slice | solution.py:16
  363.1 6.2 %constant_dynamic-slice_fusion.2 = f32[1,2048,192]{1,0,2:T(1,128)S(1)} fusion(f32[15,2048,192]{1,0,2:T(8,128)} %get-tuple-element.184, s32[]{:T(128)S(6)} %copy.121), kind=kLoop, calls=%fused_computation.14.clone.1 | loop fusion | bytes 3145732 | tf_op jit(solution)/shard_map/while/body/jit(dynamic_index_in_dim)/dynamic_slice | solution.py:16
  382.3 6.2 %constant_dynamic-slice_fusion.2 = f32[1,2048,192]{1,0,2:T(1,128)S(1)} fusion(f32[15,2048,192]{1,0,2:T(8,128)} %get-tuple-element.184, s32[]{:T(128)S(6)} %copy.121), kind=kLoop, calls=%fused_computation.14.clone.1 | loop fusion | bytes 3145732 | tf_op jit(solution)/shard_map/while/body/jit(dynamic_index_in_dim)/dynamic_slice | solution.py:16
  420.7 6.2 %constant_dynamic-slice_fusion.2 = f32[1,2048,192]{1,0,2:T(1,128)S(1)} fusion(f32[15,2048,192]{1,0,2:T(8,128)} %get-tuple-element.184, s32[]{:T(128)S(6)} %copy.121), kind=kLoop, calls=%fused_computation.14.clone.1 | loop fusion | bytes 3145732 | tf_op jit(solution)/shard_map/while/body/jit(dynamic_index_in_dim)/dynamic_slice | solution.py:16
  449.5 6.2 %constant_dynamic-slice_fusion.2 = f32[1,2048,192]{1,0,2:T(1,128)S(1)} fusion(f32[15,2048,192]{1,0,2:T(8,128)} %get-tuple-element.184, s32[]{:T(128)S(6)} %copy.121), kind=kLoop, calls=%fused_computation.14.clone.1 | loop fusion | bytes 3145732 | tf_op jit(solution)/shard_map/while/body/jit(dynamic_index_in_dim)/dynamic_slice | solution.py:16
  461.5 30.2 %reduce-scatter.2.cloned.1.call-done = bf16[16,1536]{1,0:T(8,128)(2,1)} async-done(((bf16[128,1536]{1,0:T(8,128)(2,1)}), bf16[16,1536]{1,0:T(8,128)(2,1)}) %reduce-scatter.2.cloned.1.call-update) | async-done | bytes 49168 | tf_op jit(solution)/shard_map/reduce_scatter | solution.py:142
  496.6 27.0 %all_to_all.10 = bf16[32,16,1536]{2,1,0:T(8,128)(2,1)S(1)} all-to-all(bf16[32,16,1536]{2,1,0:T(8,128)(2,1)S(1)} %multiply_convert_fusion), channel_id=1, replica_groups=mesh['req'=16,'kv'=8] {'req'}, dimensions={0} | all-to-all | bytes 3145728 | tf_op jit(solution)/shard_map/all_to_all | solution.py:162
  529.4 22.3 %all_to_all.11 = bf16[32,16,1536]{2,1,0:T(8,128)(2,1)S(1)} all-to-all(bf16[32,16,1536]{2,1,0:T(8,128)(2,1)S(1)} %bitcast.109), channel_id=1, replica_groups=mesh['req'=16,'kv'=8] {'req'}, dimensions={0} | all-to-all | bytes 3145728 | tf_op jit(solution)/shard_map/all_to_all | solution.py:171
  (194 shorter events, 146.0 us)
Async XLA Ops:
  6.5 521.7 %copy-start = (bf16[2,512,1536]{2,1,0:T(8,128)(2,1)S(1)}, bf16[2,512,1536]{2,1,0:T(8,128)(2,1)}, u32[]{:S(2)}) copy-start(bf16[2,512,1536]{2,1,0:T(8,128)(2,1)} %param.30) | copy-start | bytes 9437188
  6.5 34.1 %copy-start.1 = (s32[2048]{0:T(1024)S(1)}, s32[2048]{0:T(1024)}, u32[]{:S(2)}) copy-start(s32[2048]{0:T(1024)} %param.25) | copy-start | bytes 24580
  6.5 34.1 %copy-start.13 = (s32[384]{0:T(512)S(1)}, s32[384]{0:T(512)}, u32[]{:S(2)}) copy-start(s32[384]{0:T(512)} %param.26) | copy-start | bytes 4612
  6.5 266.3 %all-gather.5.cloned.1.call-start = ((), (), s32[]{:S(2)}) async-start(), calls=%async_computation.4 | async-start | bytes 26738688 | tf_op jit(solution)/shard_map/all_gather | solution.py:13
  81.3 18.3 %copy-start.5 = (f32[384,3]{1,0:T(8,128)}, f32[384,3]{1,0:T(8,128)S(1)}, u32[]{:S(2)}) copy-start(f32[384,3]{1,0:T(8,128)S(1)} %gather_fusion.2) | copy-start | bytes 13828
  90.0 9.6 %copy-start.9 = (pred[384,128]{1,0:T(8,128)(4,1)S(1)}, pred[384,128]{1,0:T(8,128)(4,1)}, u32[]{:S(2)}) copy-start(pred[384,128]{1,0:T(8,128)(4,1)} %copy-done.8) | copy-start | bytes 147460
  117.0 25.0 %copy-start.6 = (f32[384,3]{1,0:T(8,128)S(1)}, f32[384,3]{1,0:T(8,128)}, u32[]{:S(2)}) copy-start(f32[384,3]{1,0:T(8,128)} %copy-done.5) | copy-start | bytes 13828
  117.0 374.7 %reduce-scatter.2.cloned.1.call-start = ((), (), s32[]{:S(2)}) async-start(), calls=%async_computation.3 | async-start | bytes 442368 | tf_op jit(solution)/shard_map/reduce_scatter | solution.py:142
  141.0 27.7 %copy-start.4 = (bf16[128,1536]{1,0:T(8,128)(2,1)S(1)}, bf16[128,1536]{1,0:T(8,128)(2,1)}, u32[]{:S(2)}) copy-start(bf16[128,1536]{1,0:T(8,128)(2,1)} %param.17) | copy-start | bytes 1179652
  141.0 27.7 %copy-start.14 = (bf16[64,1536]{1,0:T(8,128)(2,1)S(1)}, bf16[64,1536]{1,0:T(8,128)(2,1)}, u32[]{:S(2)}) copy-start(bf16[64,1536]{1,0:T(8,128)(2,1)} %param.21) | copy-start | bytes 589828
  141.0 27.7 %copy-start.15 = (f32[1536]{0:T(1024)S(1)}, f32[1536]{0:T(1024)}, u32[]{:S(2)}) copy-start(f32[1536]{0:T(1024)} %param.18) | copy-start | bytes 18436
  141.0 27.7 %copy-start.17 = (f32[128]{0:T(128)S(1)}, f32[128]{0:T(128)}, u32[]{:S(2)}) copy-start(f32[128]{0:T(128)} %copy-done.16) | copy-start | bytes 1540
  314.1 147.1 %copy-start.10 = (s32[16,8]{0,1:T(8,128)S(1)}, s32[16,8]{0,1:T(8,128)}, u32[]{:S(2)}) copy-start(s32[16,8]{0,1:T(8,128)} %param.31) | copy-start | bytes 1540
  314.1 178.5 %copy-start.11 = (bf16[1536,32]{0,1:T(8,128)(2,1)S(1)}, bf16[1536,32]{0,1:T(8,128)(2,1)}, u32[]{:S(2)}) copy-start(bf16[1536,32]{0,1:T(8,128)(2,1)} %param.28) | copy-start | bytes 294916
  314.1 178.5 %copy-start.12 = (f32[1536]{0:T(1024)S(1)}, f32[1536]{0:T(1024)}, u32[]{:S(2)}) copy-start(f32[1536]{0:T(1024)} %param.27) | copy-start | bytes 18436
  314.1 7.2 %copy-start.2 = (f32[2048,192]{0,1:T(8,128)S(1)}, f32[2048,192]{0,1:T(8,128)}, u32[]{:S(2)}) copy-start(f32[2048,192]{0,1:T(8,128)} %get-tuple-element.173) | copy-start | bytes 4718596 | tf_op jit(solution)/shard_map/while
  323.7 7.2 %copy-start.2 = (f32[2048,192]{0,1:T(8,128)S(1)}, f32[2048,192]{0,1:T(8,128)}, u32[]{:S(2)}) copy-start(f32[2048,192]{0,1:T(8,128)} %get-tuple-element.173) | copy-start | bytes 4718596 | tf_op jit(solution)/shard_map/while
  333.3 7.2 %copy-start.2 = (f32[2048,192]{0,1:T(8,128)S(1)}, f32[2048,192]{0,1:T(8,128)}, u32[]{:S(2)}) copy-start(f32[2048,192]{0,1:T(8,128)} %get-tuple-element.173) | copy-start | bytes 4718596 | tf_op jit(solution)/shard_map/while
  342.9 7.2 %copy-start.2 = (f32[2048,192]{0,1:T(8,128)S(1)}, f32[2048,192]{0,1:T(8,128)}, u32[]{:S(2)}) copy-start(f32[2048,192]{0,1:T(8,128)} %get-tuple-element.173) | copy-start | bytes 4718596 | tf_op jit(solution)/shard_map/while
  352.5 7.2 %copy-start.2 = (f32[2048,192]{0,1:T(8,128)S(1)}, f32[2048,192]{0,1:T(8,128)}, u32[]{:S(2)}) copy-start(f32[2048,192]{0,1:T(8,128)} %get-tuple-element.173) | copy-start | bytes 4718596 | tf_op jit(solution)/shard_map/while
  362.1 7.2 %copy-start.2 = (f32[2048,192]{0,1:T(8,128)S(1)}, f32[2048,192]{0,1:T(8,128)}, u32[]{:S(2)}) copy-start(f32[2048,192]{0,1:T(8,128)} %get-tuple-element.173) | copy-start | bytes 4718596 | tf_op jit(solution)/shard_map/while
  371.7 7.2 %copy-start.2 = (f32[2048,192]{0,1:T(8,128)S(1)}, f32[2048,192]{0,1:T(8,128)}, u32[]{:S(2)}) copy-start(f32[2048,192]{0,1:T(8,128)} %get-tuple-element.173) | copy-start | bytes 4718596 | tf_op jit(solution)/shard_map/while
  381.3 7.2 %copy-start.2 = (f32[2048,192]{0,1:T(8,128)S(1)}, f32[2048,192]{0,1:T(8,128)}, u32[]{:S(2)}) copy-start(f32[2048,192]{0,1:T(8,128)} %get-tuple-element.173) | copy-start | bytes 4718596 | tf_op jit(solution)/shard_map/while
  390.9 7.2 %copy-start.2 = (f32[2048,192]{0,1:T(8,128)S(1)}, f32[2048,192]{0,1:T(8,128)}, u32[]{:S(2)}) copy-start(f32[2048,192]{0,1:T(8,128)} %get-tuple-element.173) | copy-start | bytes 4718596 | tf_op jit(solution)/shard_map/while
  (24 other events, 72.5 us)
Sparse Core Ops, SparseCore 0:
  117.1 155.6 all-gather.4
  461.3 30.2 reduce-scatter.1
where the time goes:
time: 570 us; the launch traced here: 562 us
  local copies, waits for them, and re-layouts  207 us (36%)
  waiting for transfers between devices  134 us (24%)
  blocking collectives  124 us (22%)
  other arithmetic  45 us (8%)
  matrix products  38 us (7%)
  between operations  13.7 us (2%)
    all_gather x1, waiting for transfers between devices, merged_2(): pieces = jax.tree.map(lambda part: lax.all_gather(part, axis), value)  104 us
    dynamic_slice x15, local copies, waits for them, and re-layouts, merged_2(): lax.scan(lambda so_far, share: (join(so_far, share), None), head, tail)  93.6 us
    all_gather x2, blocking collectives, merged_2(): pieces = jax.tree.map(lambda part: lax.all_gather(part, axis), value)  46.3 us
    slice x4, local copies, waits for them, and re-layouts, merged_2(): tail = jax.tree.map(lambda part: part[1:], pieces)  40.3 us
    reduce_scatter x1, waiting for transfers between devices, shards(): lax.psum_scatter(projected.astype(jnp.bfloat16), 'kv', scatter_dimension=...  30.2 us
    all_gather x1, blocking collectives, shards(): lax.all_gather(query.reshape(row_count, heads_dev * HD), 'req', axis=0, t...  28.5 us
    all_to_all x1, blocking collectives, shards(): lax.all_to_all(outgoing, 'req', split_axis=0, concat_axis=0, tiled=True)  27 us
    all_to_all x1, blocking collectives, shards(): lax.all_to_all(produced, 'req', split_axis=0, concat_axis=0, tiled=True)  22.3 us
  transfers between devices with their start and end apart: 2, of which 2 were waited for; matrix products, arithmetic and copies ran while one was open for 1% of the time, Pallas kernels for 0%

commit v1 on v0

v1 whole, which is shorter than its diff:
```python
import jax
import jax.numpy as jnp
from jax import lax
from jax.experimental import pallas as pl
from jax.experimental.pallas import tpu as pltpu
from jax.sharding import PartitionSpec as P

HD = 64
FFE = 512
BLK = 128
PAGES = 3
PAD = 32
LOW = -1e30
MESH = pl.DeviceIdType.MESH
F32 = jnp.float32
BF16 = jnp.bfloat16


def dot_nt(left, right):
    return lax.dot_general(left, right, (((1,), (1,)), ((), ())), preferred_element_type=F32)


def dot_nn(left, right):
    return jnp.dot(left, right, preferred_element_type=F32)


def iota(shape, axis):
    return lax.broadcasted_iota(jnp.int32, shape, axis)


def split_3(value):
    high = value.astype(BF16).astype(F32)
    rest = value - high
    middle = rest.astype(BF16).astype(F32)
    return high, middle, rest - middle


def kernel(
    hidden_hbm, gain_ref, wq_hbm, wk_hbm, wv_hbm, wout_hbm, k_hbm, v_hbm, lens_ref, slots_ref,
    moe_gain_ref, router_ref, up_hbm, down_hbm, routes_ref,
    out_ref,
    hid, wqkv, wout, kbuf, vbuf, up, down,
    pm_send, pm_recv, q_send, q_recv, q6, thr, part, part_send, part_recv, gather_t,
    rotated, value_new, proj, proj_recv, tok_send, tok, act, mixed, mixed_send, mixed_recv,
    local_sem, send_sem, recv_sem,
):
    me = lax.axis_index("req")
    kv = lax.axis_index("kv")
    mz, mx = me // 4, me % 4
    n_req, n_kv = 16, 8
    rows, model = hid.shape
    blocks = kbuf.shape[0]

    loads = [
        (hidden_hbm, hid), (wq_hbm, wqkv.at[pl.ds(0, 192)]), (wk_hbm, wqkv.at[pl.ds(192, 64)]),
        (wv_hbm, wqkv.at[pl.ds(256, 64)]), (k_hbm, kbuf), (v_hbm, vbuf), (wout_hbm, wout),
        (up_hbm, up), (down_hbm, down),
    ]
    loads = [
        pltpu.make_async_copy(src, dst, local_sem.at[i]) for i, (src, dst) in enumerate(loads)
    ]
    for load in loads:
        load.start()

    def req_peer(o):
        return ((mz + o // 4) % 4) * 4 + (mx + o % 4) % 4

    def kv_peer(o):
        return (kv + o) % n_kv

    barrier = pltpu.get_barrier_semaphore()

    def greet_req(o, carry):
        pl.semaphore_signal(barrier, inc=1, device_id={"req": req_peer(o)}, device_id_type=MESH)
        return carry

    def greet_kv(o, carry):
        pl.semaphore_signal(barrier, inc=1, device_id={"kv": kv_peer(o)}, device_id_type=MESH)
        return carry

    lax.fori_loop(1, n_req, greet_req, 0)
    lax.fori_loop(1, n_kv, greet_kv, 0)

    def remote(phase, o, axis, source, target):
        peer = req_peer(o) if axis == "req" else kv_peer(o)
        return pltpu.make_async_remote_copy(
            src_ref=source(peer), dst_ref=target, send_sem=send_sem.at[phase, o],
            recv_sem=recv_sem.at[phase, o], device_id={axis: peer}, device_id_type=MESH,
        )

    def start_all(phase, count, axis, source, target):
        def body(o, carry):
            remote(phase, o, axis, source, target).start()
            return carry

        lax.fori_loop(1, count, body, 0)

    def wait_recv_all(phase, count, axis, source, target):
        def body(o, carry):
            remote(phase, o, axis, source, target).wait_recv()
            return carry

        lax.fori_loop(1, count, body, 0)

    def wait_send_all(phase, count, axis, source, target):
        def body(o, carry):
            remote(phase, o, axis, source, target).wait_send()
            return carry

        lax.fori_loop(1, count, body, 0)

    eye = iota((128, 128), 0) == iota((128, 128), 1)

    def column(row):
        return jnp.sum(jnp.where(eye, row, 0.0), 1, keepdims=True)

    slots = slots_ref[...]
    owner = (slots * 43691) >> 17
    page = slots - owner * PAGES
    home = owner >> 7
    place = page * 128 + (owner & 127)
    home_f = home.astype(F32)
    place_f = place.astype(F32)
    home_row = jnp.concatenate([home_f[i : i + 1] for i in range(3)], 1)
    place_row = jnp.concatenate([place_f[i : i + 1] for i in range(3)], 1)
    home_col = jnp.concatenate([column(home_f[i : i + 1]) for i in range(3)], 0)
    place_col = jnp.concatenate([column(place_f[i : i + 1]) for i in range(3)], 0)
    home_hot = (home_row == iota((16, blocks), 0).astype(F32)).astype(F32).astype(BF16)
    place_hot = (place_col == iota((blocks, blocks), 1).astype(F32)).astype(F32).astype(BF16)
    present = dot_nn(home_hot, place_hot)
    pm_send[...] = jnp.zeros_like(pm_send)
    for j in range(PAGES):
        pm_send[:, j, :] = present[:, 128 * j : 128 * (j + 1)]

    pl.semaphore_wait(barrier, n_req + n_kv - 2)
    presence = (0, n_req, "req", lambda peer: pm_send.at[peer], pm_recv.at[me])
    start_all(*presence)
    pm_recv[pl.ds(me, 1)] = pm_send[pl.ds(me, 1)]

    order_row = home_row * 384.0 + place_row
    order_col = home_col * 384.0 + place_col
    before = (order_col < order_row).astype(F32)
    slot_row = jnp.sum(before, 0, keepdims=True) + 8.0 * home_row
    after = (order_row < order_col).astype(F32)
    slot_col = jnp.sum(after, 1, keepdims=True) + 8.0 * home_col
    n_slot = n_req * PAD

    len_row = lens_ref[pl.ds(me, 1), :].astype(F32)
    len_col = column(len_row)
    lane = iota((rows, 256), 1)
    frequency = jnp.exp((lane & 31).astype(F32) * (-9.210340371976184 / 32.0))
    angles = len_col * frequency
    cosines = jnp.cos(angles)
    sines = jnp.sin(angles)
    upper = (lane & 63) >= 32
    for load in loads[:4]:
        load.wait()
    values = hid[...].astype(F32)
    scale = lax.rsqrt(jnp.mean(values * values, -1, keepdims=True) + 1e-05)
    normed = (values * scale * gain_ref[...]).astype(BF16)
    qk = dot_nt(normed, wqkv[pl.ds(0, 256), :])
    value_new[...] = dot_nt(normed, wqkv[pl.ds(256, 64), :]).astype(BF16)
    swapped = jnp.where(upper, pltpu.roll(qk, 32, 1), pltpu.roll(qk, 224, 1))
    turned = qk * cosines + jnp.where(upper, swapped, -swapped) * sines
    turned = jnp.where(lane < 192, turned * 0.125, turned).astype(BF16)
    rotated[...] = turned

    wait_recv_all(*presence)
    held = pm_recv[...].reshape(128, 128)
    held_b = held.astype(BF16)
    r0, c0 = iota((128, 128), 0), iota((128, 128), 1)
    ahead = (r0 < c0).astype(F32).astype(BF16)
    earlier = (((r0 >> 3) == (c0 >> 3)) & (c0 < r0)).astype(F32).astype(BF16)
    ones = jnp.ones((128, 128), BF16)
    counts = dot_nn(held_b, ahead) + dot_nn(dot_nn(earlier, held_b).astype(BF16), ones)
    source_slot = held * (counts + ((r0 >> 3) * PAD).astype(F32))
    page_slot = jnp.sum(source_slot.reshape(16, 8, 128), 0)
    page_row = jnp.concatenate([page_slot[j : j + 1] for j in range(PAGES)], 1)
    page_col = jnp.concatenate([column(page_slot[j : j + 1]) for j in range(PAGES)], 0)
    pick = (iota((n_slot, blocks), 0).astype(F32) == page_row).astype(F32).astype(BF16)
    gather_t[...] = (iota((blocks, n_slot), 1).astype(F32) == page_col).astype(F32).astype(BF16)
    extended = []
    for j in range(PAGES):
        used = jnp.clip(len_col - 128.0 * j, 0.0, 128.0)
        extended.append(jnp.where(lane < 192, turned.astype(F32), used).astype(BF16))
    q_send[...] = dot_nn(pick, jnp.concatenate(extended, 0)).astype(BF16)

    def slot_rows(index):
        return pl.ds(pl.multiple_of(index * PAD, PAD), PAD)

    queries = (1, n_req, "req", lambda peer: q_send.at[slot_rows(peer)], q_recv.at[slot_rows(me)])
    start_all(*queries)
    q_recv[slot_rows(me), :] = q_send[slot_rows(me), :]
    place_slot = (slot_col == iota((blocks, n_slot), 1).astype(F32)).astype(F32).astype(BF16)
    wait_recv_all(*queries)
    arrived = dot_nn(place_slot, q_recv[...])
    zeros = jnp.zeros((blocks, HD), BF16)
    for q in range(3):
        head = arrived[:, HD * q : HD * (q + 1)].astype(BF16)
        q6[q] = jnp.concatenate([head, zeros], 1)
        q6[q + 3] = jnp.concatenate([zeros, head], 1)
    limit = arrived[:, 192:256]
    thr[...] = jnp.concatenate([limit, limit], 1)

    loads[4].wait()
    loads[5].wait()
    wide_r, wide_c = iota((96, 256), 0), iota((96, 256), 1)
    position = jnp.where((wide_r & 15) == (wide_c & 15), 2 * (wide_c >> 4), 1 << 20).astype(F32)
    stat_lane = iota((16, HD), 1)

    def one_group(g):
        here = pl.ds(pl.multiple_of(g * 16, 16), 16)
        query = q6[:, here, :].reshape(96, 128)
        bound = thr[here, :]
        bound = jnp.concatenate([bound] * 3 + [bound - 1.0] * 3, 0)
        bound = jnp.concatenate([bound, bound], 1)
        scores = []
        for c in range(4):
            keys = jnp.concatenate(
                [kbuf[here, 128 * i : 128 * (i + 1)] for i in range(16 * c, 16 * c + 16)], 0
            )
            scores.append(jnp.where(position < bound - 32.0 * c, dot_nt(query, keys), LOW))
        top = jnp.maximum(jnp.maximum(scores[0], scores[1]), jnp.maximum(scores[2], scores[3]))
        top = jnp.max(top, 1, keepdims=True)
        top = jnp.maximum(jnp.maximum(top[:48], top[48:]), -1e29)
        top_2 = jnp.concatenate([top, top], 0)
        weights = [jnp.exp(s - top_2) for s in scores]
        total = jnp.sum((weights[0] + weights[1]) + (weights[2] + weights[3]), 1, keepdims=True)
        total = total[:48] + total[48:]
        numer = jnp.zeros((96, 128), F32)
        for c in range(4):
            vals = jnp.concatenate(
                [vbuf[here, 128 * i : 128 * (i + 1)] for i in range(16 * c, 16 * c + 16)], 0
            )
            numer = numer + dot_nn(weights[c].astype(BF16), vals)
        numer = numer[:48, :HD] + numer[48:, HD:]
        some = total > 0.0
        safe = jnp.where(some, total, 1.0)
        numer = numer / safe
        lse = jnp.where(some, top + jnp.log(safe), LOW)
        pieces = [numer[16 * q : 16 * (q + 1)] for q in range(3)]
        stats = jnp.zeros((16, HD), F32)
        for q in range(3):
            for t, term in enumerate(split_3(lse[16 * q : 16 * (q + 1)])):
                stats = jnp.where(stat_lane == 16 * t + q, term, stats)
        part[here, :] = jnp.concatenate(pieces + [stats], 1).astype(BF16)

    def group_step(step, carry):
        for k in range(2):
            one_group(step * 2 + k)
        return carry

    lax.fori_loop(0, blocks // 32, group_step, 0)

    slot_place = (iota((n_slot, blocks), 0).astype(F32) == slot_row).astype(F32).astype(BF16)
    part_send[...] = dot_nn(slot_place, part[...]).astype(BF16)
    partials = (
        2, n_req, "req", lambda peer: part_send.at[slot_rows(peer)], part_recv.at[slot_rows(me)],
    )
    start_all(*partials)
    part_recv[slot_rows(me), :] = part_send[slot_rows(me), :]
    own_q = rotated[...].astype(F32)
    own_k = own_q[:, 192:256]
    own_v = value_new[...].astype(F32)
    own_score = [
        jnp.sum(own_q[:, HD * q : HD * (q + 1)] * own_k, 1, keepdims=True) for q in range(3)
    ]
    wait_recv_all(*partials)
    pages = dot_nn(gather_t[...], part_recv[...])
    attended = []
    for q in range(3):
        lses, outs = [own_score[q]], [own_v]
        for j in range(PAGES):
            piece = pages[128 * j : 128 * (j + 1)]
            lses.append(
                piece[:, 192 + q : 193 + q]
                + piece[:, 208 + q : 209 + q]
                + piece[:, 224 + q : 225 + q]
            )
            outs.append(piece[:, HD * q : HD * (q + 1)])
        peak = jnp.maximum(jnp.maximum(lses[0], lses[1]), jnp.maximum(lses[2], lses[3]))
        shares = [jnp.exp(value - peak) for value in lses]
        whole = (shares[0] + shares[1]) + (shares[2] + shares[3])
        summed = shares[0] * outs[0] + shares[1] * outs[1]
        summed = summed + shares[2] * outs[2] + shares[3] * outs[3]
        attended.append((summed / whole).astype(BF16))
    attended = jnp.concatenate(attended, 1)

    loads[6].wait()
    for n in range(0, model, 512):
        proj[:, n : n + 512] = dot_nn(attended, wout[:, n : n + 512]).astype(BF16)

    def token_rows(index):
        return pl.ds(pl.multiple_of(index * 16, 16), 16)

    sums = (3, n_kv, "kv", lambda peer: proj.at[token_rows(peer)], proj_recv.at[kv])
    start_all(*sums)
    proj_recv[pl.ds(kv, 1)] = proj[token_rows(kv), :].reshape(1, 16, model)
    expert_lane = iota((16, 128), 1)
    chosen = jnp.zeros((16, 128), F32)
    for k in range(8):
        chosen = chosen + (routes_ref[:, k : k + 1] == expert_lane).astype(F32)
    wait_recv_all(*sums)
    after_attn = hid[token_rows(kv), :].astype(F32)
    total = proj_recv[0].astype(F32)
    for k in range(1, n_kv):
        total = total + proj_recv[k].astype(F32)
    after_attn = after_attn + total
    scale = lax.rsqrt(jnp.mean(after_attn * after_attn, -1, keepdims=True) + 1e-05)
    moe_in = (after_attn * scale * moe_gain_ref[...]).astype(BF16)
    logits = dot_nt(moe_in, router_ref[...])
    logits = jnp.concatenate([logits] * 4, 1)
    logits = jnp.where(chosen > 0.0, logits, LOW)
    gates = jnp.exp(logits - jnp.max(logits, 1, keepdims=True))
    gates = gates / jnp.sum(gates, 1, keepdims=True)
    high, middle, low = split_3(gates)
    tok_send[:, :model] = moe_in
    tok_send[:, model:] = jnp.concatenate(
        [high[:, :32], middle[:, :32], low[:, :32], jnp.zeros((16, 32), F32)], 1
    ).astype(BF16)

    tokens = (4, n_req, "req", lambda peer: tok_send, tok.at[token_rows(me)])
    start_all(*tokens)
    tok[token_rows(me), :] = tok_send[...]
    loads[7].wait()
    loads[8].wait()
    wait_recv_all(*tokens)
    gate_all = tok[:, model:].astype(F32)
    gate_lane = iota((256, 128), 1)
    for e in range(2):
        def up_step(f, carry):
            at_gate = pl.ds(pl.multiple_of(f * 256, 256), 256)
            at_up = pl.ds(pl.multiple_of(FFE + f * 256, 256), 256)
            gate = dot_nn(tok[:, :model], up[e, :, at_gate])
            lift = dot_nn(tok[:, :model], up[e, :, at_up])
            act[:, at_gate] = (gate * jax.nn.sigmoid(gate) * lift).astype(BF16)
            return carry

        lax.fori_loop(0, 2, up_step, 0)
        index = 2 * me + e
        mine = ((gate_lane & 31) == index) & (gate_lane < 96)
        weight = jnp.sum(jnp.where(mine, gate_all, 0.0), 1, keepdims=True)

        def down_step(n, carry):
            here = pl.ds(pl.multiple_of(n * 256, 256), 256)
            made = dot_nn(act[...], down[e, :, here]).astype(BF16).astype(F32) * weight
            if e == 0:
                mixed[:, here] = made
            else:
                mixed_send[:, here] = (mixed[:, here] + made).astype(BF16)
            return carry

        lax.fori_loop(0, model // 256, down_step, 0)
    backs = (
        5, n_req, "req", lambda peer: mixed_send.at[token_rows(peer)], mixed_recv.at[me],
    )
    start_all(*backs)
    mixed_recv[pl.ds(me, 1)] = mixed_send[token_rows(me), :].reshape(1, 16, model)
    wait_recv_all(*backs)
    result = mixed_recv[0].astype(F32)
    for d in range(1, n_req):
        result = result + mixed_recv[d].astype(F32)
    out_ref[...] = (after_attn + result).astype(BF16)
    for exchange in (presence, queries, partials, sums, tokens, backs):
        wait_send_all(*exchange)


def shards(
    hidden_in, attn_gain, w_query, w_key, w_value, w_out, k_cache, v_cache, cache_len, block_slot,
    moe_gain, w_router, w_gate_up, w_down, routes,
):
    any_spec = pl.BlockSpec(memory_space=pl.ANY)
    vmem = pl.BlockSpec(memory_space=pltpu.VMEM)
    blocks = k_cache.shape[0]
    model = hidden_in.shape[1]
    rows = hidden_in.shape[0]
    n_slot = 16 * PAD
    scratch = [
        ((rows, model), BF16), ((320, model), BF16), ((192, model), BF16),
        ((blocks, 8192), BF16), ((blocks, 8192), BF16),
        (w_gate_up.shape, BF16), (w_down.shape, BF16),
        ((16, 8, 128), F32), ((16, 8, 128), F32),
        ((n_slot, 256), BF16), ((n_slot, 256), BF16),
        ((6, blocks, 128), BF16), ((blocks, 128), F32),
        ((blocks, 256), BF16), ((n_slot, 256), BF16), ((n_slot, 256), BF16),
        ((blocks, n_slot), BF16),
        ((rows, 256), BF16), ((rows, HD), BF16), ((rows, model), BF16), ((8, 16, model), BF16),
        ((16, model + 128), BF16), ((256, model + 128), BF16),
        ((256, FFE), BF16), ((256, model), F32), ((256, model), BF16), ((16, 16, model), BF16),
    ]
    return pl.pallas_call(
        kernel,
        out_shape=jax.ShapeDtypeStruct((16, model), BF16),
        in_specs=[
            any_spec, vmem, any_spec, any_spec, any_spec, any_spec, any_spec, any_spec, vmem, vmem,
            vmem, vmem, any_spec, any_spec, vmem,
        ],
        out_specs=vmem,
        scratch_shapes=[pltpu.VMEM(shape, dtype) for shape, dtype in scratch]
        + [
            pltpu.SemaphoreType.DMA((9,)),
            pltpu.SemaphoreType.DMA((6, 16)),
            pltpu.SemaphoreType.DMA((6, 16)),
        ],
        compiler_params=pltpu.CompilerParams(
            collective_id=0, has_side_effects=True, vmem_limit_bytes=56 << 20
        ),
    )(
        hidden_in, attn_gain.reshape(1, model), w_query, w_key, w_value, w_out,
        k_cache.reshape(blocks, 8192), v_cache.reshape(blocks, 8192),
        cache_len.reshape(16, 128), block_slot.reshape(3, 128),
        moe_gain.reshape(1, model), w_router.T, w_gate_up, w_down, routes,
    )


def solution(mesh):
    placed = (
        P("req", None),
        P(),
        P("kv", None),
        P("kv", None),
        P("kv", None),
        P("kv", None),
        P("req", "kv", None),
        P("req", "kv", None),
        P(),
        P("req"),
        P(),
        P(),
        P("req", None, None),
        P("req", None, None),
        P(("req", "kv"), None),
    )
    return jax.shard_map(
        shards, mesh=mesh, in_specs=placed, out_specs=P(("req", "kv"), None), check_vma=False
    )
```

time: 570 us -> 88.2 us (0.15); the launches traced: 562 us -> 87.9 us
  local copies, waits for them, and re-layouts: 207 us -> 5.36 us
  waiting for transfers between devices: 134 us -> 0 us
  blocking collectives: 124 us -> 0 us
  Pallas kernels: 0 us -> 82.5 us
  other arithmetic: 45 us -> 0 us
  matrix products: 38 us -> 0 us
  between operations: 13.7 us -> 0.01 us
    all_gather x1 -> x0, waiting for transfers between devices: 104 us -> none  [merged_2(): pieces = jax.tree.map(lambda part: lax.all_gather(part, axis), value)]
    dynamic_slice x15 -> x0, local copies, waits for them, and re-layouts: 93.6 us -> none  [merged_2(): lax.scan(lambda so_far, share: (join(so_far, share), None), head, tail)]
    pallas_call x0 -> x1, Pallas kernels: none -> 82.5 us  [shards(): pl.pallas_call(kernel, out_shape=jax.ShapeDtypeStruct((16, model), BF16),...]
    all_gather x3 -> x0, blocking collectives: 74.7 us -> none  [the longest x2 46.3 us: merged_2(): pieces = jax.tree.map(lambda part: lax.all_gather(part, axis), value)]
    all_to_all x2 -> x0, blocking collectives: 49.3 us -> none  [the longest x1 27 us: shards(): lax.all_to_all(outgoing, 'req', split_axis=0, concat_axis=0, tiled=True)]
    slice x7 -> x0, local copies, waits for them, and re-layouts: 43 us -> none  [the longest x4 40.3 us: merged_2(): tail = jax.tree.map(lambda part: part[1:], pieces)]
    dot_general x12 -> x0, matrix products: 38 us -> none  [the longest x1 12.9 us: shards(): jnp.einsum('bgqt,bgtd->bgqd', weights, cache_values, precision=lax.Precis...]
    add x31 -> x0, other arithmetic: 32.9 us -> none  [the longest x15 18.6 us: blend_parts(): first_numer + second_numer]
  transfers between devices with their start and end apart: 2 -> 0, of which waited for: 2 -> 0; matrix products, arithmetic and copies ran while one was open for 1% -> 0% of each run, Pallas kernels for 0% -> 0%
where the time goes in v1:
time: 88.2 us; the launch traced here: 87.9 us
  Pallas kernels  82.5 us (94%)
  local copies, waits for them, and re-layouts  5.36 us (6%)
    pallas_call x1, Pallas kernels, shards(): pl.pallas_call(kernel, out_shape=jax.ShapeDtypeStruct((16, model), BF16),...  82.5 us
    unnamed x2, local copies, waits for them, and re-layouts  2.78 us

profile of v1, /device:TPU:0, one launch (start us, length us, event | category | flops | bytes accessed | tf_op | source)
XLA Modules:
  0.0 87.9 jit_solution(16167461764506464044)
XLA Ops:
  0.0 1.3 %reshape.18.gain_ref = f32[1,1536]{1,0:T(1,128)} reshape(f32[1536]{0:T(1024)} %param.16) | data formatting | bytes 12288 | tf_op jit(solution)/shard_map/reshape | solution.py:409
  1.3 1.3 %reshape.23.moe_gain_ref = f32[1,1536]{1,0:T(1,128)} reshape(f32[1536]{0:T(1024)} %param.25) | data formatting | bytes 12288 | tf_op jit(solution)/shard_map/reshape | solution.py:412
  2.6 1.4 %copy.16.routes_ref = s32[16,8]{1,0:T(8,128)} copy(s32[16,8]{0,1:T(8,128)} %param.29) | data formatting | bytes 1024 | tf_op args[14]
  3.9 82.5 %shard_map.145 = bf16[16,1536]{1,0:T(8,128)(2,1)} custom-call(bf16[128,1536]{1,0:T(8,128)(2,1)} %hidden_hbm.1, f32[1,1536]{1,0:T(1,128)} %reshape.18.gain_ref, bf16[192,1536]{1,0:T(8,128)(2,1)} %wq_hbm.1, bf16[64,1536]{1,0:T(8,128)(2,1)} %wk_hbm.1, bf16[64,1536]{1,0:T(8,128)(2,1)} %wv_hbm.1, bf16[192,1536]{1,0:T(8,128)(2,1)} %wout_hbm.1, ...), custom_call_target="tpu_custom_call" | custom-call | tf_op jit(solution)/shard_map/pallas_call | solution.py:391
  86.4 1.4 %copy.18 = bf16[16,1536]{1,0:T(8,128)(2,1)} copy(bf16[16,1536]{1,0:T(8,128)(2,1)} %shard_map.145) | data formatting | bytes 98304

commit v2 on v1

--- a/solution.py
+++ b/solution.py
@@ -10,6 +10,7 @@
 BLK = 128
 PAGES = 3
 PAD = 32
+CHUNK = 64
 LOW = -1e30
 MESH = pl.DeviceIdType.MESH
 F32 = jnp.float32
@@ -41,7 +42,8 @@
     out_ref,
     hid, wqkv, wout, kbuf, vbuf, up, down,
     pm_send, pm_recv, q_send, q_recv, q6, thr, part, part_send, part_recv, gather_t,
-    rotated, value_new, proj, proj_recv, tok_send, tok, act, mixed, mixed_send, mixed_recv,
+    rotated, value_new, proj, proj_recv, att, att_peer, wout_peer,
+    tok_send, tok, mixed, mixed_send, mixed_recv,
     local_sem, send_sem, recv_sem,
 ):
     me = lax.axis_index("req")
@@ -65,9 +67,6 @@
     def req_peer(o):
         return ((mz + o // 4) % 4) * 4 + (mx + o % 4) % 4
 
-    def kv_peer(o):
-        return (kv + o) % n_kv
-
     barrier = pltpu.get_barrier_semaphore()
 
     def greet_req(o, carry):
@@ -75,17 +74,28 @@
         return carry
 
     def greet_kv(o, carry):
-        pl.semaphore_signal(barrier, inc=1, device_id={"kv": kv_peer(o)}, device_id_type=MESH)
+        peer = (kv + 2 * o) % n_kv
+        pl.semaphore_signal(barrier, inc=1, device_id={"kv": peer}, device_id_type=MESH)
         return carry
 
     lax.fori_loop(1, n_req, greet_req, 0)
-    lax.fori_loop(1, n_kv, greet_kv, 0)
+    lax.fori_loop(1, 4, greet_kv, 0)
+    pl.semaphore_signal(
+        barrier, inc=1, device_id={"kv": kv + 1 - 2 * (kv % 2)}, device_id_type=MESH
+    )
 
     def remote(phase, o, axis, source, target):
-        peer = req_peer(o) if axis == "req" else kv_peer(o)
+        if axis == "req":
+            name, peer = "req", req_peer(o)
+        elif axis == "core":
+            name, peer = "kv", kv + 1 - 2 * (kv % 2)
+        else:
+            name, peer = "kv", (kv + 2 * o) % n_kv
+        if axis == "y":
+            target = target.at[o]
         return pltpu.make_async_remote_copy(
             src_ref=source(peer), dst_ref=target, send_sem=send_sem.at[phase, o],
-            recv_sem=recv_sem.at[phase, o], device_id={axis: peer}, device_id_type=MESH,
+            recv_sem=recv_sem.at[phase, o], device_id={name: peer}, device_id_type=MESH,
         )
 
     def start_all(phase, count, axis, source, target):
@@ -113,6 +123,9 @@
 
     def column(row):
         return jnp.sum(jnp.where(eye, row, 0.0), 1, keepdims=True)
+
+    def wide_row(ref):
+        return jnp.concatenate([ref[i : i + 1, :] for i in range(ref.shape[0])], 1)
 
     slots = slots_ref[...]
     owner = (slots * 43691) >> 17
@@ -132,7 +145,7 @@
     for j in range(PAGES):
         pm_send[:, j, :] = present[:, 128 * j : 128 * (j + 1)]
 
-    pl.semaphore_wait(barrier, n_req + n_kv - 2)
+    pl.semaphore_wait(barrier, n_req + 3)
     presence = (0, n_req, "req", lambda peer: pm_send.at[peer], pm_recv.at[me])
     start_all(*presence)
     pm_recv[pl.ds(me, 1)] = pm_send[pl.ds(me, 1)]
@@ -157,7 +170,7 @@
         load.wait()
     values = hid[...].astype(F32)
     scale = lax.rsqrt(jnp.mean(values * values, -1, keepdims=True) + 1e-05)
-    normed = (values * scale * gain_ref[...]).astype(BF16)
+    normed = (values * scale * wide_row(gain_ref)).astype(BF16)
     qk = dot_nt(normed, wqkv[pl.ds(0, 256), :])
     value_new[...] = dot_nt(normed, wqkv[pl.ds(256, 64), :]).astype(BF16)
     swapped = jnp.where(upper, pltpu.roll(qk, 32, 1), pltpu.roll(qk, 224, 1))
@@ -190,6 +203,9 @@
 
     queries = (1, n_req, "req", lambda peer: q_send.at[slot_rows(peer)], q_recv.at[slot_rows(me)])
     start_all(*queries)
+    loads[6].wait()
+    share_w = remote(0, 0, "core", lambda peer: wout, wout_peer)
+    share_w.start()
     q_recv[slot_rows(me), :] = q_send[slot_rows(me), :]
     place_slot = (slot_col == iota((blocks, n_slot), 1).astype(F32)).astype(F32).astype(BF16)
     wait_recv_all(*queries)
@@ -208,49 +224,53 @@
     position = jnp.where((wide_r & 15) == (wide_c & 15), 2 * (wide_c >> 4), 1 << 20).astype(F32)
     stat_lane = iota((16, HD), 1)
 
-    def one_group(g):
-        here = pl.ds(pl.multiple_of(g * 16, 16), 16)
-        query = q6[:, here, :].reshape(96, 128)
-        bound = thr[here, :]
-        bound = jnp.concatenate([bound] * 3 + [bound - 1.0] * 3, 0)
-        bound = jnp.concatenate([bound, bound], 1)
+    def some_groups(step, carry):
+        at = [pl.ds(pl.multiple_of((step * 4 + k) * 16, 16), 16) for k in range(4)]
         scores = []
-        for c in range(4):
-            keys = jnp.concatenate(
-                [kbuf[here, 128 * i : 128 * (i + 1)] for i in range(16 * c, 16 * c + 16)], 0
-            )
-            scores.append(jnp.where(position < bound - 32.0 * c, dot_nt(query, keys), LOW))
-        top = jnp.maximum(jnp.maximum(scores[0], scores[1]), jnp.maximum(scores[2], scores[3]))
-        top = jnp.max(top, 1, keepdims=True)
-        top = jnp.maximum(jnp.maximum(top[:48], top[48:]), -1e29)
-        top_2 = jnp.concatenate([top, top], 0)
-        weights = [jnp.exp(s - top_2) for s in scores]
-        total = jnp.sum((weights[0] + weights[1]) + (weights[2] + weights[3]), 1, keepdims=True)
-        total = total[:48] + total[48:]
-        numer = jnp.zeros((96, 128), F32)
-        for c in range(4):
-            vals = jnp.concatenate(
-                [vbuf[here, 128 * i : 128 * (i + 1)] for i in range(16 * c, 16 * c + 16)], 0
-            )
-            numer = numer + dot_nn(weights[c].astype(BF16), vals)
-        numer = numer[:48, :HD] + numer[48:, HD:]
-        some = total > 0.0
-        safe = jnp.where(some, total, 1.0)
-        numer = numer / safe
-        lse = jnp.where(some, top + jnp.log(safe), LOW)
-        pieces = [numer[16 * q : 16 * (q + 1)] for q in range(3)]
-        stats = jnp.zeros((16, HD), F32)
-        for q in range(3):
-            for t, term in enumerate(split_3(lse[16 * q : 16 * (q + 1)])):
-                stats = jnp.where(stat_lane == 16 * t + q, term, stats)
-        part[here, :] = jnp.concatenate(pieces + [stats], 1).astype(BF16)
-
-    def group_step(step, carry):
-        for k in range(2):
-            one_group(step * 2 + k)
+        for here in at:
+            query = q6[:, here, :].reshape(96, 128)
+            bound = thr[here, :]
+            bound = jnp.concatenate([bound] * 3 + [bound - 1.0] * 3, 0)
+            bound = jnp.concatenate([bound, bound], 1)
+            mine = []
+            for c in range(4):
+                keys = jnp.concatenate(
+                    [kbuf[here, 128 * i : 128 * (i + 1)] for i in range(16 * c, 16 * c + 16)], 0
+                )
+                mine.append(jnp.where(position < bound - 32.0 * c, dot_nt(query, keys), LOW))
+            scores.append(mine)
+        tops, weights, totals = [], [], []
+        for mine in scores:
+            top = jnp.maximum(jnp.maximum(mine[0], mine[1]), jnp.maximum(mine[2], mine[3]))
+            top = jnp.max(top, 1, keepdims=True)
+            top = jnp.maximum(jnp.maximum(top[:48], top[48:]), -1e29)
+            top_2 = jnp.concatenate([top, top], 0)
+            these = [jnp.exp(s - top_2) for s in mine]
+            total = jnp.sum((these[0] + these[1]) + (these[2] + these[3]), 1, keepdims=True)
+            tops.append(top)
+            weights.append([w.astype(BF16) for w in these])
+            totals.append(total[:48] + total[48:])
+        for here, top, these, total in zip(at, tops, weights, totals):
+            numer = jnp.zeros((96, 128), F32)
+            for c in range(4):
+                vals = jnp.concatenate(
+                    [vbuf[here, 128 * i : 128 * (i + 1)] for i in range(16 * c, 16 * c + 16)], 0
+                )
+                numer = numer + dot_nn(these[c], vals)
+            numer = numer[:48, :HD] + numer[48:, HD:]
+            some = total > 0.0
+            safe = jnp.where(some, total, 1.0)
+            numer = numer / safe
+            lse = jnp.where(some, top + jnp.log(safe), LOW)
+            pieces = [numer[16 * q : 16 * (q + 1)] for q in range(3)]
+            stats = jnp.zeros((16, HD), F32)
+            for q in range(3):
+                for t, term in enumerate(split_3(lse[16 * q : 16 * (q + 1)])):
+                    stats = jnp.where(stat_lane == 16 * t + q, term, stats)
+            part[here, :] = jnp.concatenate(pieces + [stats], 1).astype(BF16)
         return carry
 
-    lax.fori_loop(0, blocks // 32, group_step, 0)
+    lax.fori_loop(0, blocks // (16 * 4), some_groups, 0)
 
     slot_place = (iota((n_slot, blocks), 0).astype(F32) == slot_row).astype(F32).astype(BF16)
     part_send[...] = dot_nn(slot_place, part[...]).astype(BF16)
@@ -286,28 +306,38 @@
         attended.append((summed / whole).astype(BF16))
     attended = jnp.concatenate(attended, 1)
 
-    loads[6].wait()
-    for n in range(0, model, 512):
-        proj[:, n : n + 512] = dot_nn(attended, wout[:, n : n + 512]).astype(BF16)
+    core = kv % 2
+    att[...] = jnp.concatenate([attended, jnp.zeros((rows, HD), BF16)], 1).reshape(4, 2, 16, 256)
+    swap = remote(3, 0, "core", lambda peer: att.at[:, 1 - core], att_peer)
+    swap.start()
 
     def token_rows(index):
         return pl.ds(pl.multiple_of(index * 16, 16), 16)
 
-    sums = (3, n_kv, "kv", lambda peer: proj.at[token_rows(peer)], proj_recv.at[kv])
+    own_rows = att[:, pl.ds(core, 1)].reshape(64, 256)[:, :192]
+    share_w.wait_recv()
+    swap.wait_recv()
+    peer_rows = att_peer[...].reshape(64, 256)[:, :192]
+    for n in range(0, model, 512):
+        part_n = dot_nn(own_rows, wout[:, n : n + 512]) + dot_nn(peer_rows, wout_peer[:, n : n + 512])
+        proj[:, :, n : n + 512] = part_n.astype(BF16).reshape(4, 16, 512)
+    sums = (3, 4, "y", lambda peer: proj.at[peer // 2], proj_recv)
     start_all(*sums)
-    proj_recv[pl.ds(kv, 1)] = proj[token_rows(kv), :].reshape(1, 16, model)
-    expert_lane = iota((16, 128), 1)
-    chosen = jnp.zeros((16, 128), F32)
+    expert_row = iota((128, 16), 0)
+    chosen = jnp.zeros((128, 16), F32)
     for k in range(8):
-        chosen = chosen + (routes_ref[:, k : k + 1] == expert_lane).astype(F32)
+        chosen = chosen + (routes_ref[k : k + 1, :] == expert_row).astype(F32)
+    eye_16 = (iota((16, 16), 0) == iota((16, 16), 1)).astype(F32).astype(BF16)
+    chosen = dot_nt(eye_16, chosen.astype(BF16))
+    own_proj = proj[pl.ds(kv // 2, 1)].reshape(16, model).astype(F32)
     wait_recv_all(*sums)
     after_attn = hid[token_rows(kv), :].astype(F32)
-    total = proj_recv[0].astype(F32)
-    for k in range(1, n_kv):
+    total = own_proj
+    for k in range(1, 4):
         total = total + proj_recv[k].astype(F32)
     after_attn = after_attn + total
     scale = lax.rsqrt(jnp.mean(after_attn * after_attn, -1, keepdims=True) + 1e-05)
-    moe_in = (after_attn * scale * moe_gain_ref[...]).astype(BF16)
+    moe_in = (after_attn * scale * wide_row(moe_gain_ref)).astype(BF16)
     logits = dot_nt(moe_in, router_ref[...])
     logits = jnp.concatenate([logits] * 4, 1)
     logits = jnp.where(chosen > 0.0, logits, LOW)
@@ -319,49 +349,76 @@
         [high[:, :32], middle[:, :32], low[:, :32], jnp.zeros((16, 32), F32)], 1
     ).astype(BF16)
 
-    tokens = (4, n_req, "req", lambda peer: tok_send, tok.at[token_rows(me)])
-    start_all(*tokens)
-    tok[token_rows(me), :] = tok_send[...]
+    def offset(s):
+        k = s // 4
+        return k + (k // 2) * (5 - 2 * k), s % 4
+
+    def token_copy(s):
+        oz, ox = offset(s)
+        return pltpu.make_async_remote_copy(
+            src_ref=tok_send, dst_ref=tok.at[token_rows(s)], send_sem=send_sem.at[4, s],
+            recv_sem=recv_sem.at[4, s],
+            device_id={"req": ((mz + oz) % 4) * 4 + (mx + ox) % 4}, device_id_type=MESH,
+        )
+
+    def back_copy(s):
+        oz, ox = offset(s)
+        return pltpu.make_async_remote_copy(
+            src_ref=mixed_send.at[token_rows(s)], dst_ref=mixed_recv.at[s],
+            send_sem=send_sem.at[5, s], recv_sem=recv_sem.at[5, s],
+            device_id={"req": ((mz - oz + 4) % 4) * 4 + (mx - ox + 4) % 4}, device_id_type=MESH,
+        )
+
+    def each(first, last, action):
+        def body(s, carry):
+            action(s)
+            return carry
+
+        lax.fori_loop(first, last, body, 0)
+
+    each(1, n_req, lambda s: token_copy(s).start())
+    tok[0:16, :] = tok_send[...]
     loads[7].wait()
     loads[8].wait()
-    wait_recv_all(*tokens)
-    gate_all = tok[:, model:].astype(F32)
-    gate_lane = iota((256, 128), 1)
-    for e in range(2):
-        def up_step(f, carry):
-            at_gate = pl.ds(pl.multiple_of(f * 256, 256), 256)
-            at_up = pl.ds(pl.multiple_of(FFE + f * 256, 256), 256)
-            gate = dot_nn(tok[:, :model], up[e, :, at_gate])
-            lift = dot_nn(tok[:, :model], up[e, :, at_up])
-            act[:, at_gate] = (gate * jax.nn.sigmoid(gate) * lift).astype(BF16)
-            return carry
-
-        lax.fori_loop(0, 2, up_step, 0)
-        index = 2 * me + e
-        mine = ((gate_lane & 31) == index) & (gate_lane < 96)
-        weight = jnp.sum(jnp.where(mine, gate_all, 0.0), 1, keepdims=True)
-
-        def down_step(n, carry):
-            here = pl.ds(pl.multiple_of(n * 256, 256), 256)
-            made = dot_nn(act[...], down[e, :, here]).astype(BF16).astype(F32) * weight
-            if e == 0:
-                mixed[:, here] = made
-            else:
-                mixed_send[:, here] = (mixed[:, here] + made).astype(BF16)
-            return carry
-
-        lax.fori_loop(0, model // 256, down_step, 0)
-    backs = (
-        5, n_req, "req", lambda peer: mixed_send.at[token_rows(peer)], mixed_recv.at[me],
-    )
-    start_all(*backs)
-    mixed_recv[pl.ds(me, 1)] = mixed_send[token_rows(me), :].reshape(1, 16, model)
-    wait_recv_all(*backs)
-    result = mixed_recv[0].astype(F32)
+    gate_lane = iota((CHUNK, 128), 1)
+
+    def chunk_step(k, carry):
+        first, last = lax.max(k * (CHUNK // 16), 1), (k + 1) * (CHUNK // 16)
+        each(first, last, lambda s: token_copy(s).wait_recv())
+        here = pl.ds(pl.multiple_of(k * CHUNK, CHUNK), CHUNK)
+        inputs = tok[here, :model]
+        gate_all = tok[here, model:].astype(F32)
+        outs = []
+        for e in range(2):
+            acts = []
+            for f in range(0, FFE, 256):
+                gate = dot_nn(inputs, up[e, :, f : f + 256])
+                lift = dot_nn(inputs, up[e, :, FFE + f : FFE + f + 256])
+                acts.append((gate * jax.nn.sigmoid(gate) * lift).astype(BF16))
+            act = jnp.concatenate(acts, 1)
+            mine = ((gate_lane & 31) == 2 * me + e) & (gate_lane < 96)
+            weight = jnp.sum(jnp.where(mine, gate_all, 0.0), 1, keepdims=True)
+            for n in range(0, model, 256):
+                made = dot_nn(act, down[e, :, n : n + 256]).astype(BF16).astype(F32) * weight
+                if e == 0:
+                    mixed[:, n : n + 256] = made
+                else:
+                    made = mixed[:, n : n + 256] + made
+                    mixed_send[here, n : n + 256] = made.astype(BF16)
+        each(first, last, lambda s: back_copy(s).start())
+        return carry
+
+    lax.fori_loop(0, 256 // CHUNK, chunk_step, 0)
+    result = mixed_send[0:16, :].astype(F32)
+    each(1, n_req, lambda s: back_copy(s).wait_recv())
     for d in range(1, n_req):
         result = result + mixed_recv[d].astype(F32)
     out_ref[...] = (after_attn + result).astype(BF16)
-    for exchange in (presence, queries, partials, sums, tokens, backs):
+    each(1, n_req, lambda s: token_copy(s).wait_send())
+    each(1, n_req, lambda s: back_copy(s).wait_send())
+    share_w.wait_send()
+    swap.wait_send()
+    for exchange in (presence, queries, partials, sums):
         wait_send_all(*exchange)
 
 
@@ -384,9 +441,10 @@
         ((6, blocks, 128), BF16), ((blocks, 128), F32),
         ((blocks, 256), BF16), ((n_slot, 256), BF16), ((n_slot, 256), BF16),
         ((blocks, n_slot), BF16),
-        ((rows, 256), BF16), ((rows, HD), BF16), ((rows, model), BF16), ((8, 16, model), BF16),
+        ((rows, 256), BF16), ((rows, HD), BF16), ((4, 16, model), BF16), ((4, 16, model), BF16),
+        ((4, 2, 16, 256), BF16), ((4, 16, 256), BF16), ((192, model), BF16),
         ((16, model + 128), BF16), ((256, model + 128), BF16),
-        ((256, FFE), BF16), ((256, model), F32), ((256, model), BF16), ((16, 16, model), BF16),
+        ((CHUNK, model), F32), ((256, model), BF16), ((16, 16, model), BF16),
     ]
     return pl.pallas_call(
         kernel,
@@ -406,10 +464,10 @@
             collective_id=0, has_side_effects=True, vmem_limit_bytes=56 << 20
         ),
     )(
-        hidden_in, attn_gain.reshape(1, model), w_query, w_key, w_value, w_out,
+        hidden_in, attn_gain.reshape(model // 128, 128), w_query, w_key, w_value, w_out,
         k_cache.reshape(blocks, 8192), v_cache.reshape(blocks, 8192),
         cache_len.reshape(16, 128), block_slot.reshape(3, 128),
-        moe_gain.reshape(1, model), w_router.T, w_gate_up, w_down, routes,
+        moe_gain.reshape(model // 128, 128), w_router.T, w_gate_up, w_down, routes.T,
     )
 
 

time: 88.2 us -> 70.1 us (0.79)
  Pallas kernels: 82.5 us -> 68.2 us
  local copies, waits for them, and re-layouts: 5.36 us -> 1.42 us
    pallas_call x1, Pallas kernels: 82.5 us -> 68.2 us  [shards(): pl.pallas_call(kernel, out_shape=jax.ShapeDtypeStruct((16, model), BF16),...]
    reshape x2 -> x0, local copies, waits for them, and re-layouts: 2.58 us -> none  [the longest x1 1.29 us: shards(): attn_gain.reshape(1, model)]
    unnamed x2 -> x1, local copies, waits for them, and re-layouts: 2.78 us -> 1.42 us
where the time goes in v2:
time: 70.1 us; the launch traced here: 69.7 us
  Pallas kernels  68.2 us (97%)
  local copies, waits for them, and re-layouts  1.42 us (2%)
    pallas_call x1, Pallas kernels, shards(): pl.pallas_call(kernel, out_shape=jax.ShapeDtypeStruct((16, model), BF16),...  68.2 us
    unnamed x1, local copies, waits for them, and re-layouts  1.42 us

profile of v2, /device:TPU:0, one launch (start us, length us, event | category | flops | bytes accessed | tf_op | source)
XLA Modules:
  0.0 69.7 jit_solution(6759409442852092599)
XLA Ops:
  0.0 68.2 %shard_map.145 = bf16[16,1536]{1,0:T(8,128)(2,1)} custom-call(bf16[128,1536]{1,0:T(8,128)(2,1)} %hidden_hbm.1, f32[12,128]{1,0:T(8,128)} %bitcast.11, bf16[192,1536]{1,0:T(8,128)(2,1)} %wq_hbm.1, bf16[64,1536]{1,0:T(8,128)(2,1)} %wk_hbm.1, bf16[64,1536]{1,0:T(8,128)(2,1)} %wv_hbm.1, bf16[192,1536]{1,0:T(8,128)(2,1)} %wout_hbm.1, bf16[384,8192]{1,0:T(8,128)(2,1)} %bitcast.8, ...), custom_call_target="tpu_custom_call" | custom-call | tf_op jit(solution)/shard_map/pallas_call | solution.py:449
  68.2 1.4 %copy.17 = bf16[16,1536]{1,0:T(8,128)(2,1)} copy(bf16[16,1536]{1,0:T(8,128)(2,1)} %shard_map.145) | data formatting | bytes 98304

commit v3 on v2

--- a/solution.py
+++ b/solution.py
@@ -11,6 +11,10 @@
 PAGES = 3
 PAD = 32
 CHUNK = 64
+ORDER = [
+    (0, 0), (0, 1), (3, 0), (0, 3), (1, 0), (0, 2), (2, 0), (1, 1),
+    (3, 3), (1, 3), (3, 1), (2, 1), (1, 2), (2, 3), (3, 2), (2, 2),
+]
 LOW = -1e30
 MESH = pl.DeviceIdType.MESH
 F32 = jnp.float32
@@ -43,7 +47,7 @@
     hid, wqkv, wout, kbuf, vbuf, up, down,
     pm_send, pm_recv, q_send, q_recv, q6, thr, part, part_send, part_recv, gather_t,
     rotated, value_new, proj, proj_recv, att, att_peer, wout_peer,
-    tok_send, tok, mixed, mixed_send, mixed_recv,
+    mask_send, mask_recv, slot_place, tok_send, tok, mixed, mixed_send, mixed_recv,
     local_sem, send_sem, recv_sem,
 ):
     me = lax.axis_index("req")
@@ -97,6 +101,36 @@
             src_ref=source(peer), dst_ref=target, send_sem=send_sem.at[phase, o],
             recv_sem=recv_sem.at[phase, o], device_id={name: peer}, device_id_type=MESH,
         )
+
+    def far_req(s):
+        oz, ox = ORDER[s]
+        return ((mz + oz) % 4) * 4 + (mx + ox) % 4
+
+    def near_req(s):
+        oz, ox = ORDER[s]
+        return ((mz + 4 - oz) % 4) * 4 + (mx + 4 - ox) % 4
+
+    def token_rows(index):
+        return pl.ds(pl.multiple_of(index * 16, 16), 16)
+
+    def slot_copy(phase, s, source, target, peer):
+        return pltpu.make_async_remote_copy(
+            src_ref=source, dst_ref=target, send_sem=send_sem.at[phase, s],
+            recv_sem=recv_sem.at[phase, s], device_id={"req": peer}, device_id_type=MESH,
+        )
+
+    def mask_copy(s):
+        return slot_copy(6, s, mask_send, mask_recv.at[pl.ds(16 * s, 16)], far_req(s))
+
+    def token_copy(s):
+        return slot_copy(4, s, tok_send, tok.at[pl.ds(16 * s, 16)], far_req(s))
+
+    def back_copy(s):
+        return slot_copy(5, s, mixed_send.at[pl.ds(16 * s, 16)], mixed_recv.at[s], near_req(s))
+
+    def each(first, last, action):
+        for s in range(first, last):
+            action(s)
 
     def start_all(phase, count, axis, source, target):
         def body(o, carry):
@@ -203,11 +237,20 @@
 
     queries = (1, n_req, "req", lambda peer: q_send.at[slot_rows(peer)], q_recv.at[slot_rows(me)])
     start_all(*queries)
+    expert_row = iota((128, 16), 0)
+    chosen = jnp.zeros((128, 16), F32)
+    for k in range(8):
+        chosen = chosen + (routes_ref[k : k + 1, :] == expert_row).astype(F32)
+    eye_16 = (iota((16, 16), 0) == iota((16, 16), 1)).astype(F32).astype(BF16)
+    mask_send[...] = dot_nt(eye_16, chosen.astype(BF16)).astype(BF16)
+    mask_recv[0:16, :] = mask_send[...]
+    each(1, n_req, lambda s: mask_copy(s).start())
     loads[6].wait()
     share_w = remote(0, 0, "core", lambda peer: wout, wout_peer)
     share_w.start()
     q_recv[slot_rows(me), :] = q_send[slot_rows(me), :]
     place_slot = (slot_col == iota((blocks, n_slot), 1).astype(F32)).astype(F32).astype(BF16)
+    slot_place[...] = (iota((n_slot, blocks), 0).astype(F32) == slot_row).astype(F32).astype(BF16)
     wait_recv_all(*queries)
     arrived = dot_nn(place_slot, q_recv[...])
     zeros = jnp.zeros((blocks, HD), BF16)
@@ -225,7 +268,7 @@
     stat_lane = iota((16, HD), 1)
 
     def some_groups(step, carry):
-        at = [pl.ds(pl.multiple_of((step * 4 + k) * 16, 16), 16) for k in range(4)]
+        at = [pl.ds(pl.multiple_of((step * 8 + k) * 16, 16), 16) for k in range(8)]
         scores = []
         for here in at:
             query = q6[:, here, :].reshape(96, 128)
@@ -270,10 +313,9 @@
             part[here, :] = jnp.concatenate(pieces + [stats], 1).astype(BF16)
         return carry
 
-    lax.fori_loop(0, blocks // (16 * 4), some_groups, 0)
-
-    slot_place = (iota((n_slot, blocks), 0).astype(F32) == slot_row).astype(F32).astype(BF16)
-    part_send[...] = dot_nn(slot_place, part[...]).astype(BF16)
+    lax.fori_loop(0, blocks // (16 * 8), some_groups, 0)
+
+    part_send[...] = dot_nn(slot_place[...], part[...]).astype(BF16)
     partials = (
         2, n_req, "req", lambda peer: part_send.at[slot_rows(peer)], part_recv.at[slot_rows(me)],
     )
@@ -311,24 +353,16 @@
     swap = remote(3, 0, "core", lambda peer: att.at[:, 1 - core], att_peer)
     swap.start()
 
-    def token_rows(index):
-        return pl.ds(pl.multiple_of(index * 16, 16), 16)
-
     own_rows = att[:, pl.ds(core, 1)].reshape(64, 256)[:, :192]
+    own_part = [dot_nn(own_rows, wout[:, n : n + 512]) for n in range(0, model, 512)]
     share_w.wait_recv()
     swap.wait_recv()
     peer_rows = att_peer[...].reshape(64, 256)[:, :192]
     for n in range(0, model, 512):
-        part_n = dot_nn(own_rows, wout[:, n : n + 512]) + dot_nn(peer_rows, wout_peer[:, n : n + 512])
+        part_n = own_part[n // 512] + dot_nn(peer_rows, wout_peer[:, n : n + 512])
         proj[:, :, n : n + 512] = part_n.astype(BF16).reshape(4, 16, 512)
     sums = (3, 4, "y", lambda peer: proj.at[peer // 2], proj_recv)
     start_all(*sums)
-    expert_row = iota((128, 16), 0)
-    chosen = jnp.zeros((128, 16), F32)
-    for k in range(8):
-        chosen = chosen + (routes_ref[k : k + 1, :] == expert_row).astype(F32)
-    eye_16 = (iota((16, 16), 0) == iota((16, 16), 1)).astype(F32).astype(BF16)
-    chosen = dot_nt(eye_16, chosen.astype(BF16))
     own_proj = proj[pl.ds(kv // 2, 1)].reshape(16, model).astype(F32)
     wait_recv_all(*sums)
     after_attn = hid[token_rows(kv), :].astype(F32)
@@ -338,66 +372,30 @@
     after_attn = after_attn + total
     scale = lax.rsqrt(jnp.mean(after_attn * after_attn, -1, keepdims=True) + 1e-05)
     moe_in = (after_attn * scale * wide_row(moe_gain_ref)).astype(BF16)
-    logits = dot_nt(moe_in, router_ref[...])
-    logits = jnp.concatenate([logits] * 4, 1)
-    logits = jnp.where(chosen > 0.0, logits, LOW)
-    gates = jnp.exp(logits - jnp.max(logits, 1, keepdims=True))
-    gates = gates / jnp.sum(gates, 1, keepdims=True)
-    high, middle, low = split_3(gates)
-    tok_send[:, :model] = moe_in
-    tok_send[:, model:] = jnp.concatenate(
-        [high[:, :32], middle[:, :32], low[:, :32], jnp.zeros((16, 32), F32)], 1
-    ).astype(BF16)
-
-    def offset(s):
-        k = s // 4
-        return k + (k // 2) * (5 - 2 * k), s % 4
-
-    def token_copy(s):
-        oz, ox = offset(s)
-        return pltpu.make_async_remote_copy(
-            src_ref=tok_send, dst_ref=tok.at[token_rows(s)], send_sem=send_sem.at[4, s],
-            recv_sem=recv_sem.at[4, s],
-            device_id={"req": ((mz + oz) % 4) * 4 + (mx + ox) % 4}, device_id_type=MESH,
-        )
-
-    def back_copy(s):
-        oz, ox = offset(s)
-        return pltpu.make_async_remote_copy(
-            src_ref=mixed_send.at[token_rows(s)], dst_ref=mixed_recv.at[s],
-            send_sem=send_sem.at[5, s], recv_sem=recv_sem.at[5, s],
-            device_id={"req": ((mz - oz + 4) % 4) * 4 + (mx - ox + 4) % 4}, device_id_type=MESH,
-        )
-
-    def each(first, last, action):
-        def body(s, carry):
-            action(s)
-            return carry
-
-        lax.fori_loop(first, last, body, 0)
-
+    tok_send[...] = moe_in
     each(1, n_req, lambda s: token_copy(s).start())
     tok[0:16, :] = tok_send[...]
     loads[7].wait()
     loads[8].wait()
     gate_lane = iota((CHUNK, 128), 1)
-
-    def chunk_step(k, carry):
-        first, last = lax.max(k * (CHUNK // 16), 1), (k + 1) * (CHUNK // 16)
+    each(1, n_req, lambda s: mask_copy(s).wait_recv())
+    for k in range(256 // CHUNK):
+        first, last = max(k * (CHUNK // 16), 1), (k + 1) * (CHUNK // 16)
         each(first, last, lambda s: token_copy(s).wait_recv())
-        here = pl.ds(pl.multiple_of(k * CHUNK, CHUNK), CHUNK)
-        inputs = tok[here, :model]
-        gate_all = tok[here, model:].astype(F32)
-        outs = []
+        here = pl.ds(k * CHUNK, CHUNK)
+        inputs = tok[here, :]
+        logits = jnp.concatenate([dot_nt(inputs, router_ref[...])] * 4, 1)
+        logits = jnp.where(mask_recv[here, :].astype(F32) > 0.0, logits, LOW)
+        gates = jnp.exp(logits - jnp.max(logits, 1, keepdims=True))
+        gates = gates / jnp.sum(gates, 1, keepdims=True)
         for e in range(2):
+            weight = jnp.sum(jnp.where(gate_lane == 2 * me + e, gates, 0.0), 1, keepdims=True)
             acts = []
             for f in range(0, FFE, 256):
                 gate = dot_nn(inputs, up[e, :, f : f + 256])
                 lift = dot_nn(inputs, up[e, :, FFE + f : FFE + f + 256])
                 acts.append((gate * jax.nn.sigmoid(gate) * lift).astype(BF16))
             act = jnp.concatenate(acts, 1)
-            mine = ((gate_lane & 31) == 2 * me + e) & (gate_lane < 96)
-            weight = jnp.sum(jnp.where(mine, gate_all, 0.0), 1, keepdims=True)
             for n in range(0, model, 256):
                 made = dot_nn(act, down[e, :, n : n + 256]).astype(BF16).astype(F32) * weight
                 if e == 0:
@@ -406,14 +404,13 @@
                     made = mixed[:, n : n + 256] + made
                     mixed_send[here, n : n + 256] = made.astype(BF16)
         each(first, last, lambda s: back_copy(s).start())
-        return carry
-
-    lax.fori_loop(0, 256 // CHUNK, chunk_step, 0)
+
     result = mixed_send[0:16, :].astype(F32)
-    each(1, n_req, lambda s: back_copy(s).wait_recv())
     for d in range(1, n_req):
+        back_copy(d).wait_recv()
         result = result + mixed_recv[d].astype(F32)
     out_ref[...] = (after_attn + result).astype(BF16)
+    each(1, n_req, lambda s: mask_copy(s).wait_send())
     each(1, n_req, lambda s: token_copy(s).wait_send())
     each(1, n_req, lambda s: back_copy(s).wait_send())
     share_w.wait_send()
@@ -443,7 +440,8 @@
         ((blocks, n_slot), BF16),
         ((rows, 256), BF16), ((rows, HD), BF16), ((4, 16, model), BF16), ((4, 16, model), BF16),
         ((4, 2, 16, 256), BF16), ((4, 16, 256), BF16), ((192, model), BF16),
-        ((16, model + 128), BF16), ((256, model + 128), BF16),
+        ((16, 128), BF16), ((256, 128), BF16), ((n_slot, blocks), BF16),
+        ((16, model), BF16), ((256, model), BF16),
         ((CHUNK, model), F32), ((256, model), BF16), ((16, 16, model), BF16),
     ]
     return pl.pallas_call(
@@ -457,8 +455,8 @@
         scratch_shapes=[pltpu.VMEM(shape, dtype) for shape, dtype in scratch]
         + [
             pltpu.SemaphoreType.DMA((9,)),
-            pltpu.SemaphoreType.DMA((6, 16)),
-            pltpu.SemaphoreType.DMA((6, 16)),
+            pltpu.SemaphoreType.DMA((7, 16)),
+            pltpu.SemaphoreType.DMA((7, 16)),
         ],
         compiler_params=pltpu.CompilerParams(
             collective_id=0, has_side_effects=True, vmem_limit_bytes=56 << 20

time: 70.1 us -> 65.3 us (0.932)
  Pallas kernels: 68.2 us -> 63.7 us
    pallas_call x1, Pallas kernels: 68.2 us -> 63.7 us  [shards(): pl.pallas_call(kernel, out_shape=jax.ShapeDtypeStruct((16, model), BF16),...]
where the time goes in v3:
time: 65.3 us; the launch traced here: 65.1 us
  Pallas kernels  63.7 us (98%)
  local copies, waits for them, and re-layouts  1.42 us (2%)
    pallas_call x1, Pallas kernels, shards(): pl.pallas_call(kernel, out_shape=jax.ShapeDtypeStruct((16, model), BF16),...  63.7 us
    unnamed x1, local copies, waits for them, and re-layouts  1.42 us

profile of v3, /device:TPU:0, one launch (start us, length us, event | category | flops | bytes accessed | tf_op | source)
XLA Modules:
  0.0 65.1 jit_solution(5721912919518972015)
XLA Ops:
  0.0 63.7 %shard_map.145 = bf16[16,1536]{1,0:T(8,128)(2,1)} custom-call(bf16[128,1536]{1,0:T(8,128)(2,1)} %hidden_hbm.1, f32[12,128]{1,0:T(8,128)} %bitcast.11, bf16[192,1536]{1,0:T(8,128)(2,1)} %wq_hbm.1, bf16[64,1536]{1,0:T(8,128)(2,1)} %wk_hbm.1, bf16[64,1536]{1,0:T(8,128)(2,1)} %wv_hbm.1, bf16[192,1536]{1,0:T(8,128)(2,1)} %wout_hbm.1, bf16[384,8192]{1,0:T(8,128)(2,1)} %bitcast.8, ...), custom_call_target="tpu_custom_call" | custom-call | tf_op jit(solution)/shard_map/pallas_call | solution.py:447
  63.7 1.4 %copy.17 = bf16[16,1536]{1,0:T(8,128)(2,1)} copy(bf16[16,1536]{1,0:T(8,128)(2,1)} %shard_map.145) | data formatting | bytes 98304

commit v4 on v3

--- a/solution.py
+++ b/solution.py
@@ -10,11 +10,13 @@
 BLK = 128
 PAGES = 3
 PAD = 32
-CHUNK = 64
 ORDER = [
-    (0, 0), (0, 1), (3, 0), (0, 3), (1, 0), (0, 2), (2, 0), (1, 1),
-    (3, 3), (1, 3), (3, 1), (2, 1), (1, 2), (2, 3), (3, 2), (2, 2),
+    (0, 0), (0, 1), (0, 3), (1, 0), (3, 0), (0, 2), (2, 0), (1, 1),
+    (3, 3), (1, 3), (3, 1), (1, 2), (3, 2), (2, 1), (2, 3), (2, 2),
 ]
+FAR = [oz * 4 + ox for oz, ox in reversed(ORDER) if (oz, ox) != (0, 0)]
+CHUNKS = [(0, 4), (4, 7), (7, 11), (11, 16)]
+X_FIRST = [(1, 1), (3, 3), (1, 2), (3, 2)]
 LOW = -1e30
 MESH = pl.DeviceIdType.MESH
 F32 = jnp.float32
@@ -73,16 +75,14 @@
 
     barrier = pltpu.get_barrier_semaphore()
 
-    def greet_req(o, carry):
+    for o in FAR:
         pl.semaphore_signal(barrier, inc=1, device_id={"req": req_peer(o)}, device_id_type=MESH)
-        return carry
 
     def greet_kv(o, carry):
         peer = (kv + 2 * o) % n_kv
         pl.semaphore_signal(barrier, inc=1, device_id={"kv": peer}, device_id_type=MESH)
         return carry
 
-    lax.fori_loop(1, n_req, greet_req, 0)
     lax.fori_loop(1, 4, greet_kv, 0)
     pl.semaphore_signal(
         barrier, inc=1, device_id={"kv": kv + 1 - 2 * (kv % 2)}, device_id_type=MESH
@@ -122,8 +122,24 @@
     def mask_copy(s):
         return slot_copy(6, s, mask_send, mask_recv.at[pl.ds(16 * s, 16)], far_req(s))
 
+    core = kv % 2
+
     def token_copy(s):
-        return slot_copy(4, s, tok_send, tok.at[pl.ds(16 * s, 16)], far_req(s))
+        oz, ox = ORDER[s]
+        if s < 7:
+            source, peer = tok_send, far_req(s)
+        else:
+            by_x, by_z = ORDER.index((0, ox)), ORDER.index((oz, 0))
+            to_z = ((mz + oz) % 4) * 4 + mx
+            to_x = mz * 4 + (mx + ox) % 4
+            if (oz, ox) == (2, 2):
+                source = tok.at[token_rows(by_x + core * (by_z - by_x))]
+                peer = to_z + core * (to_x - to_z)
+            elif (oz, ox) in X_FIRST:
+                source, peer = tok.at[token_rows(by_x)], to_z
+            else:
+                source, peer = tok.at[token_rows(by_z)], to_x
+        return slot_copy(4, s, source, tok.at[token_rows(s)], peer)
 
     def back_copy(s):
         return slot_copy(5, s, mixed_send.at[pl.ds(16 * s, 16)], mixed_recv.at[s], near_req(s))
@@ -173,23 +189,25 @@
     home_col = jnp.concatenate([column(home_f[i : i + 1]) for i in range(3)], 0)
     place_col = jnp.concatenate([column(place_f[i : i + 1]) for i in range(3)], 0)
     home_hot = (home_row == iota((16, blocks), 0).astype(F32)).astype(F32).astype(BF16)
-    place_hot = (place_col == iota((blocks, blocks), 1).astype(F32)).astype(F32).astype(BF16)
-    present = dot_nn(home_hot, place_hot)
-    pm_send[...] = jnp.zeros_like(pm_send)
-    for j in range(PAGES):
-        pm_send[:, j, :] = present[:, 128 * j : 128 * (j + 1)]
-
-    pl.semaphore_wait(barrier, n_req + 3)
-    presence = (0, n_req, "req", lambda peer: pm_send.at[peer], pm_recv.at[me])
-    start_all(*presence)
-    pm_recv[pl.ds(me, 1)] = pm_send[pl.ds(me, 1)]
-
     order_row = home_row * 384.0 + place_row
     order_col = home_col * 384.0 + place_col
     before = (order_col < order_row).astype(F32)
     slot_row = jnp.sum(before, 0, keepdims=True) + 8.0 * home_row
     after = (order_row < order_col).astype(F32)
     slot_col = jnp.sum(after, 1, keepdims=True) + 8.0 * home_col
+    rank = slot_col - PAD * home_col + 1.0
+    place_rank = jnp.where(place_col == iota((blocks, blocks), 1).astype(F32), rank, 0.0)
+    present = dot_nn(home_hot, place_rank.astype(BF16))
+    pm_send[...] = jnp.zeros_like(pm_send)
+    for j in range(PAGES):
+        pm_send[:, j, :] = present[:, 128 * j : 128 * (j + 1)]
+
+    pl.semaphore_wait(barrier, n_req + 3)
+    presence = (0, n_req, "req", lambda peer: pm_send.at[peer], pm_recv.at[me])
+    for o in FAR:
+        remote(0, o, "req", presence[3], presence[4]).start()
+    pm_recv[pl.ds(me, 1)] = pm_send[pl.ds(me, 1)]
+
     n_slot = n_req * PAD
 
     len_row = lens_ref[pl.ds(me, 1), :].astype(F32)
@@ -213,30 +231,34 @@
     rotated[...] = turned
 
     wait_recv_all(*presence)
-    held = pm_recv[...].reshape(128, 128)
-    held_b = held.astype(BF16)
-    r0, c0 = iota((128, 128), 0), iota((128, 128), 1)
-    ahead = (r0 < c0).astype(F32).astype(BF16)
-    earlier = (((r0 >> 3) == (c0 >> 3)) & (c0 < r0)).astype(F32).astype(BF16)
-    ones = jnp.ones((128, 128), BF16)
-    counts = dot_nn(held_b, ahead) + dot_nn(dot_nn(earlier, held_b).astype(BF16), ones)
-    source_slot = held * (counts + ((r0 >> 3) * PAD).astype(F32))
-    page_slot = jnp.sum(source_slot.reshape(16, 8, 128), 0)
+    held = pm_recv[...]
+    base = (iota((16, 8, 128), 0) * PAD - 1).astype(F32)
+    page_slot = jnp.sum(jnp.where(held > 0.0, held + base, 0.0), 0)
     page_row = jnp.concatenate([page_slot[j : j + 1] for j in range(PAGES)], 1)
-    page_col = jnp.concatenate([column(page_slot[j : j + 1]) for j in range(PAGES)], 0)
-    pick = (iota((n_slot, blocks), 0).astype(F32) == page_row).astype(F32).astype(BF16)
-    gather_t[...] = (iota((blocks, n_slot), 1).astype(F32) == page_col).astype(F32).astype(BF16)
     extended = []
     for j in range(PAGES):
         used = jnp.clip(len_col - 128.0 * j, 0.0, 128.0)
         extended.append(jnp.where(lane < 192, turned.astype(F32), used).astype(BF16))
-    q_send[...] = dot_nn(pick, jnp.concatenate(extended, 0)).astype(BF16)
+    extended = jnp.concatenate(extended, 0)
+
+    def z_rows(oz):
+        z = (mz + oz) % 4
+        return z, pl.ds(pl.multiple_of(z * 4 * PAD, 4 * PAD), 4 * PAD)
 
     def slot_rows(index):
         return pl.ds(pl.multiple_of(index * PAD, PAD), PAD)
 
     queries = (1, n_req, "req", lambda peer: q_send.at[slot_rows(peer)], q_recv.at[slot_rows(me)])
-    start_all(*queries)
+    for oz in (2, 1, 3, 0):
+        z, there = z_rows(oz)
+        number = (iota((4 * PAD, blocks), 0) + z * 4 * PAD).astype(F32)
+        pick = (number == page_row).astype(F32).astype(BF16)
+        q_send[there, :] = dot_nn(pick, extended).astype(BF16)
+        for ox in (2, 1, 3, 0):
+            if (oz, ox) != (0, 0):
+                remote(1, oz * 4 + ox, "req", queries[3], queries[4]).start()
+    page_col = jnp.concatenate([column(page_slot[j : j + 1]) for j in range(PAGES)], 0)
+    gather_t[...] = (iota((blocks, n_slot), 1).astype(F32) == page_col).astype(F32).astype(BF16)
     expert_row = iota((128, 16), 0)
     chosen = jnp.zeros((128, 16), F32)
     for k in range(8):
@@ -315,41 +337,43 @@
 
     lax.fori_loop(0, blocks // (16 * 8), some_groups, 0)
 
-    part_send[...] = dot_nn(slot_place[...], part[...]).astype(BF16)
     partials = (
         2, n_req, "req", lambda peer: part_send.at[slot_rows(peer)], part_recv.at[slot_rows(me)],
     )
-    start_all(*partials)
+    for oz in (2, 1, 3, 0):
+        z, there = z_rows(oz)
+        part_send[there, :] = dot_nn(slot_place[there, :], part[...]).astype(BF16)
+        for ox in (2, 1, 3, 0):
+            if (oz, ox) != (0, 0):
+                remote(2, oz * 4 + ox, "req", partials[3], partials[4]).start()
     part_recv[slot_rows(me), :] = part_send[slot_rows(me), :]
     own_q = rotated[...].astype(F32)
     own_k = own_q[:, 192:256]
     own_v = value_new[...].astype(F32)
     own_score = [
-        jnp.sum(own_q[:, HD * q : HD * (q + 1)] * own_k, 1, keepdims=True) for q in range(3)
+        jnp.broadcast_to(
+            jnp.sum(own_q[:, HD * q : HD * (q + 1)] * own_k, 1, keepdims=True), (rows, HD)
+        )
+        for q in range(3)
     ]
+    own_score = jnp.concatenate(own_score + [jnp.zeros((rows, HD), F32)], 1)
+    own_v = jnp.concatenate([own_v] * 4, 1)
+    spread_r, spread_c = iota((HD, 256), 0), iota((HD, 256), 1)
+    spread = ((spread_r & 15) == (spread_c >> 6)) & (spread_r < 48) & (spread_c < 192)
+    spread = spread.astype(F32).astype(BF16)
     wait_recv_all(*partials)
     pages = dot_nn(gather_t[...], part_recv[...])
-    attended = []
-    for q in range(3):
-        lses, outs = [own_score[q]], [own_v]
-        for j in range(PAGES):
-            piece = pages[128 * j : 128 * (j + 1)]
-            lses.append(
-                piece[:, 192 + q : 193 + q]
-                + piece[:, 208 + q : 209 + q]
-                + piece[:, 224 + q : 225 + q]
-            )
-            outs.append(piece[:, HD * q : HD * (q + 1)])
-        peak = jnp.maximum(jnp.maximum(lses[0], lses[1]), jnp.maximum(lses[2], lses[3]))
-        shares = [jnp.exp(value - peak) for value in lses]
-        whole = (shares[0] + shares[1]) + (shares[2] + shares[3])
-        summed = shares[0] * outs[0] + shares[1] * outs[1]
-        summed = summed + shares[2] * outs[2] + shares[3] * outs[3]
-        attended.append((summed / whole).astype(BF16))
-    attended = jnp.concatenate(attended, 1)
-
-    core = kv % 2
-    att[...] = jnp.concatenate([attended, jnp.zeros((rows, HD), BF16)], 1).reshape(4, 2, 16, 256)
+    lses = dot_nn(pages[:, 192:256].astype(BF16), spread)
+    lses = [own_score] + [lses[128 * j : 128 * (j + 1)] for j in range(PAGES)]
+    outs = [own_v] + [pages[128 * j : 128 * (j + 1)] for j in range(PAGES)]
+    peak = jnp.maximum(jnp.maximum(lses[0], lses[1]), jnp.maximum(lses[2], lses[3]))
+    shares = [jnp.exp(value - peak) for value in lses]
+    whole = (shares[0] + shares[1]) + (shares[2] + shares[3])
+    summed = shares[0] * outs[0] + shares[1] * outs[1]
+    summed = summed + shares[2] * outs[2] + shares[3] * outs[3]
+    attended = summed / whole
+    attended = jnp.where(lane < 192, attended, 0.0).astype(BF16)
+    att[...] = attended.reshape(4, 2, 16, 256)
     swap = remote(3, 0, "core", lambda peer: att.at[:, 1 - core], att_peer)
     swap.start()
 
@@ -373,16 +397,23 @@
     scale = lax.rsqrt(jnp.mean(after_attn * after_attn, -1, keepdims=True) + 1e-05)
     moe_in = (after_attn * scale * wide_row(moe_gain_ref)).astype(BF16)
     tok_send[...] = moe_in
-    each(1, n_req, lambda s: token_copy(s).start())
+    each(1, 7, lambda s: token_copy(s).start())
     tok[0:16, :] = tok_send[...]
+    for s in range(1, 7):
+        token_copy(s).wait_recv()
+        for t in range(7, 16):
+            oz, ox = ORDER[t]
+            ready = {1: [(1, 1)], 2: [(3, 3)], 3: [(1, 3)], 4: [(3, 1)], 5: [(1, 2), (3, 2)]}
+            if (oz, ox) in ready.get(s, [(2, 1), (2, 3), (2, 2)]):
+                token_copy(t).start()
     loads[7].wait()
     loads[8].wait()
-    gate_lane = iota((CHUNK, 128), 1)
     each(1, n_req, lambda s: mask_copy(s).wait_recv())
-    for k in range(256 // CHUNK):
-        first, last = max(k * (CHUNK // 16), 1), (k + 1) * (CHUNK // 16)
-        each(first, last, lambda s: token_copy(s).wait_recv())
-        here = pl.ds(k * CHUNK, CHUNK)
+    for first, last in CHUNKS:
+        each(max(first, 7), last, lambda s: token_copy(s).wait_recv())
+        count = 16 * (last - first)
+        here = pl.ds(16 * first, count)
+        gate_lane = iota((count, 128), 1)
         inputs = tok[here, :]
         logits = jnp.concatenate([dot_nt(inputs, router_ref[...])] * 4, 1)
         logits = jnp.where(mask_recv[here, :].astype(F32) > 0.0, logits, LOW)
@@ -399,11 +430,11 @@
             for n in range(0, model, 256):
                 made = dot_nn(act, down[e, :, n : n + 256]).astype(BF16).astype(F32) * weight
                 if e == 0:
-                    mixed[:, n : n + 256] = made
+                    mixed[0:count, n : n + 256] = made
                 else:
-                    made = mixed[:, n : n + 256] + made
+                    made = mixed[0:count, n : n + 256] + made
                     mixed_send[here, n : n + 256] = made.astype(BF16)
-        each(first, last, lambda s: back_copy(s).start())
+        each(max(first, 1), last, lambda s: back_copy(s).start())
 
     result = mixed_send[0:16, :].astype(F32)
     for d in range(1, n_req):
@@ -442,7 +473,7 @@
         ((4, 2, 16, 256), BF16), ((4, 16, 256), BF16), ((192, model), BF16),
         ((16, 128), BF16), ((256, 128), BF16), ((n_slot, blocks), BF16),
         ((16, model), BF16), ((256, model), BF16),
-        ((CHUNK, model), F32), ((256, model), BF16), ((16, 16, model), BF16),
+        ((80, model), F32), ((256, model), BF16), ((16, 16, model), BF16),
     ]
     return pl.pallas_call(
         kernel,

time: 65.3 us -> 62.3 us (0.954)
  Pallas kernels: 63.7 us -> 60.7 us
    pallas_call x1, Pallas kernels: 63.7 us -> 60.7 us  [shards(): pl.pallas_call(kernel, out_shape=jax.ShapeDtypeStruct((16, model), BF16),...]
where the time goes in v4:
time: 62.3 us; the launch traced here: 62.2 us
  Pallas kernels  60.7 us (97%)
  local copies, waits for them, and re-layouts  1.42 us (2%)
    pallas_call x1, Pallas kernels, shards(): pl.pallas_call(kernel, out_shape=jax.ShapeDtypeStruct((16, model), BF16),...  60.7 us
    unnamed x1, local copies, waits for them, and re-layouts  1.42 us

profile of v4, /device:TPU:0, one launch (start us, length us, event | category | flops | bytes accessed | tf_op | source)
XLA Modules:
  0.0 62.2 jit_solution(3473877051586223149)
XLA Ops:
  0.0 60.7 %shard_map.145 = bf16[16,1536]{1,0:T(8,128)(2,1)} custom-call(bf16[128,1536]{1,0:T(8,128)(2,1)} %hidden_hbm.1, f32[12,128]{1,0:T(8,128)} %bitcast.11, bf16[192,1536]{1,0:T(8,128)(2,1)} %wq_hbm.1, bf16[64,1536]{1,0:T(8,128)(2,1)} %wk_hbm.1, bf16[64,1536]{1,0:T(8,128)(2,1)} %wv_hbm.1, bf16[192,1536]{1,0:T(8,128)(2,1)} %wout_hbm.1, bf16[384,8192]{1,0:T(8,128)(2,1)} %bitcast.8, ...), custom_call_target="tpu_custom_call" | custom-call | tf_op jit(solution)/shard_map/pallas_call | solution.py:478
  60.7 1.4 %copy.17 = bf16[16,1536]{1,0:T(8,128)(2,1)} copy(bf16[16,1536]{1,0:T(8,128)(2,1)} %shard_map.145) | data formatting | bytes 98304

commit v5 on v4

--- a/solution.py
+++ b/solution.py
@@ -10,13 +10,15 @@
 BLK = 128
 PAGES = 3
 PAD = 32
+SHARE = 24
 ORDER = [
-    (0, 0), (0, 1), (0, 3), (1, 0), (3, 0), (0, 2), (2, 0), (1, 1),
-    (3, 3), (1, 3), (3, 1), (1, 2), (3, 2), (2, 1), (2, 3), (2, 2),
+    (0, 0), (0, 2), (2, 0), (0, 1), (0, 3), (1, 0), (3, 0),
+    (1, 1), (3, 3), (1, 3), (3, 1), (1, 2), (3, 2), (2, 1), (2, 3), (2, 2),
 ]
 FAR = [oz * 4 + ox for oz, ox in reversed(ORDER) if (oz, ox) != (0, 0)]
-CHUNKS = [(0, 4), (4, 7), (7, 11), (11, 16)]
-X_FIRST = [(1, 1), (3, 3), (1, 2), (3, 2)]
+CHUNKS = [(0, 7), (7, 11), (11, 16)]
+DIRECT = 11
+X_FIRST = [(1, 2), (3, 2)]
 LOW = -1e30
 MESH = pl.DeviceIdType.MESH
 F32 = jnp.float32
@@ -43,9 +45,10 @@
 
 
 def kernel(
-    hidden_hbm, gain_ref, wq_hbm, wk_hbm, wv_hbm, wout_hbm, k_hbm, v_hbm, lens_ref, slots_ref,
-    moe_gain_ref, router_ref, up_hbm, down_hbm, routes_ref,
+    hidden_hbm, gain_hbm, wq_hbm, wk_hbm, wv_hbm, wout_hbm, k_hbm, v_hbm, lens_hbm, slots_hbm,
+    moe_gain_hbm, router_hbm, up_hbm, down_hbm, routes_hbm,
     out_ref,
+    gain_ref, lens_ref, slots_ref, moe_gain_ref, router_ref, routes_ref,
     hid, wqkv, wout, kbuf, vbuf, up, down,
     pm_send, pm_recv, q_send, q_recv, q6, thr, part, part_send, part_recv, gather_t,
     rotated, value_new, proj, proj_recv, att, att_peer, wout_peer,
@@ -59,6 +62,24 @@
     rows, model = hid.shape
     blocks = kbuf.shape[0]
 
+    def req_peer(o):
+        return ((mz + o // 4) % 4) * 4 + (mx + o % 4) % 4
+
+    barrier = pltpu.get_barrier_semaphore()
+
+    for o in FAR:
+        pl.semaphore_signal(barrier, inc=1, device_id={"req": req_peer(o)}, device_id_type=MESH)
+
+    def greet_kv(o, carry):
+        peer = (kv + 2 * o) % n_kv
+        pl.semaphore_signal(barrier, inc=1, device_id={"kv": peer}, device_id_type=MESH)
+        return carry
+
+    lax.fori_loop(1, 4, greet_kv, 0)
+    pl.semaphore_signal(
+        barrier, inc=1, device_id={"kv": kv + 1 - 2 * (kv % 2)}, device_id_type=MESH
+    )
+
     loads = [
         (hidden_hbm, hid), (wq_hbm, wqkv.at[pl.ds(0, 192)]), (wk_hbm, wqkv.at[pl.ds(192, 64)]),
         (wv_hbm, wqkv.at[pl.ds(256, 64)]), (k_hbm, kbuf), (v_hbm, vbuf), (wout_hbm, wout),
@@ -67,26 +88,17 @@
     loads = [
         pltpu.make_async_copy(src, dst, local_sem.at[i]) for i, (src, dst) in enumerate(loads)
     ]
-    for load in loads:
+    smalls = [
+        (slots_hbm, slots_ref), (lens_hbm, lens_ref), (gain_hbm, gain_ref),
+        (moe_gain_hbm, moe_gain_ref), (router_hbm, router_ref), (routes_hbm, routes_ref),
+    ]
+    smalls = [
+        pltpu.make_async_copy(src, dst, local_sem.at[9 + i]) for i, (src, dst) in enumerate(smalls)
+    ]
+    for load in smalls + loads[:7]:
         load.start()
-
-    def req_peer(o):
-        return ((mz + o // 4) % 4) * 4 + (mx + o % 4) % 4
-
-    barrier = pltpu.get_barrier_semaphore()
-
-    for o in FAR:
-        pl.semaphore_signal(barrier, inc=1, device_id={"req": req_peer(o)}, device_id_type=MESH)
-
-    def greet_kv(o, carry):
-        peer = (kv + 2 * o) % n_kv
-        pl.semaphore_signal(barrier, inc=1, device_id={"kv": peer}, device_id_type=MESH)
-        return carry
-
-    lax.fori_loop(1, 4, greet_kv, 0)
-    pl.semaphore_signal(
-        barrier, inc=1, device_id={"kv": kv + 1 - 2 * (kv % 2)}, device_id_type=MESH
-    )
+    for load in smalls:
+        load.wait()
 
     def remote(phase, o, axis, source, target):
         if axis == "req":
@@ -126,7 +138,7 @@
 
     def token_copy(s):
         oz, ox = ORDER[s]
-        if s < 7:
+        if s < DIRECT:
             source, peer = tok_send, far_req(s)
         else:
             by_x, by_z = ORDER.index((0, ox)), ORDER.index((oz, 0))
@@ -199,6 +211,8 @@
     place_rank = jnp.where(place_col == iota((blocks, blocks), 1).astype(F32), rank, 0.0)
     present = dot_nn(home_hot, place_rank.astype(BF16))
     pm_send[...] = jnp.zeros_like(pm_send)
+    q_recv[...] = jnp.zeros_like(q_recv)
+    part_recv[...] = jnp.zeros_like(part_recv)
     for j in range(PAGES):
         pm_send[:, j, :] = present[:, 128 * j : 128 * (j + 1)]
 
@@ -246,7 +260,7 @@
         return z, pl.ds(pl.multiple_of(z * 4 * PAD, 4 * PAD), 4 * PAD)
 
     def slot_rows(index):
-        return pl.ds(pl.multiple_of(index * PAD, PAD), PAD)
+        return pl.ds(pl.multiple_of(index * PAD, PAD), SHARE)
 
     queries = (1, n_req, "req", lambda peer: q_send.at[slot_rows(peer)], q_recv.at[slot_rows(me)])
     for oz in (2, 1, 3, 0):
@@ -267,6 +281,8 @@
     mask_send[...] = dot_nt(eye_16, chosen.astype(BF16)).astype(BF16)
     mask_recv[0:16, :] = mask_send[...]
     each(1, n_req, lambda s: mask_copy(s).start())
+    loads[7].start()
+    loads[8].start()
     loads[6].wait()
     share_w = remote(0, 0, "core", lambda peer: wout, wout_peer)
     share_w.start()
@@ -397,20 +413,17 @@
     scale = lax.rsqrt(jnp.mean(after_attn * after_attn, -1, keepdims=True) + 1e-05)
     moe_in = (after_attn * scale * wide_row(moe_gain_ref)).astype(BF16)
     tok_send[...] = moe_in
-    each(1, 7, lambda s: token_copy(s).start())
+    each(1, DIRECT, lambda s: token_copy(s).start())
     tok[0:16, :] = tok_send[...]
-    for s in range(1, 7):
+    for s, onward in ((1, [(1, 2), (3, 2)]), (2, [(2, 1), (2, 3), (2, 2)])):
         token_copy(s).wait_recv()
-        for t in range(7, 16):
-            oz, ox = ORDER[t]
-            ready = {1: [(1, 1)], 2: [(3, 3)], 3: [(1, 3)], 4: [(3, 1)], 5: [(1, 2), (3, 2)]}
-            if (oz, ox) in ready.get(s, [(2, 1), (2, 3), (2, 2)]):
-                token_copy(t).start()
+        for place in onward:
+            token_copy(ORDER.index(place)).start()
     loads[7].wait()
     loads[8].wait()
     each(1, n_req, lambda s: mask_copy(s).wait_recv())
     for first, last in CHUNKS:
-        each(max(first, 7), last, lambda s: token_copy(s).wait_recv())
+        each(max(first, 3), last, lambda s: token_copy(s).wait_recv())
         count = 16 * (last - first)
         here = pl.ds(16 * first, count)
         gate_lane = iota((count, 128), 1)
@@ -473,19 +486,21 @@
         ((4, 2, 16, 256), BF16), ((4, 16, 256), BF16), ((192, model), BF16),
         ((16, 128), BF16), ((256, 128), BF16), ((n_slot, blocks), BF16),
         ((16, model), BF16), ((256, model), BF16),
-        ((80, model), F32), ((256, model), BF16), ((16, 16, model), BF16),
+        ((112, model), F32), ((256, model), BF16), ((16, 16, model), BF16),
     ]
     return pl.pallas_call(
         kernel,
         out_shape=jax.ShapeDtypeStruct((16, model), BF16),
-        in_specs=[
-            any_spec, vmem, any_spec, any_spec, any_spec, any_spec, any_spec, any_spec, vmem, vmem,
-            vmem, vmem, any_spec, any_spec, vmem,
-        ],
+        in_specs=[any_spec] * 15,
         out_specs=vmem,
-        scratch_shapes=[pltpu.VMEM(shape, dtype) for shape, dtype in scratch]
+        scratch_shapes=[
+            pltpu.VMEM((model // 128, 128), F32), pltpu.VMEM((16, 128), jnp.int32),
+            pltpu.VMEM((3, 128), jnp.int32), pltpu.VMEM((model // 128, 128), F32),
+            pltpu.VMEM((32, model), BF16), pltpu.VMEM((8, 16), jnp.int32),
+        ]
+        + [pltpu.VMEM(shape, dtype) for shape, dtype in scratch]
         + [
-            pltpu.SemaphoreType.DMA((9,)),
+            pltpu.SemaphoreType.DMA((15,)),
             pltpu.SemaphoreType.DMA((7, 16)),
             pltpu.SemaphoreType.DMA((7, 16)),
         ],

time: 62.3 us -> 60 us (0.963)
  Pallas kernels: 60.7 us -> 58.4 us
    pallas_call x1, Pallas kernels: 60.7 us -> 58.4 us  [shards(): pl.pallas_call(kernel, out_shape=jax.ShapeDtypeStruct((16, model), BF16),...]
where the time goes in v5:
time: 60 us; the launch traced here: 59.8 us
  Pallas kernels  58.4 us (97%)
  local copies, waits for them, and re-layouts  1.42 us (2%)
    pallas_call x1, Pallas kernels, shards(): pl.pallas_call(kernel, out_shape=jax.ShapeDtypeStruct((16, model), BF16),...  58.4 us
    unnamed x1, local copies, waits for them, and re-layouts  1.42 us

profile of v5, /device:TPU:0, one launch (start us, length us, event | category | flops | bytes accessed | tf_op | source)
XLA Modules:
  0.0 59.8 jit_solution(4050119129480854979)
XLA Ops:
  0.0 58.4 %shard_map.145 = bf16[16,1536]{1,0:T(8,128)(2,1)} custom-call(bf16[128,1536]{1,0:T(8,128)(2,1)} %hidden_hbm.1, f32[12,128]{1,0:T(8,128)} %bitcast.11, bf16[192,1536]{1,0:T(8,128)(2,1)} %wq_hbm.1, bf16[64,1536]{1,0:T(8,128)(2,1)} %wk_hbm.1, bf16[64,1536]{1,0:T(8,128)(2,1)} %wv_hbm.1, bf16[192,1536]{1,0:T(8,128)(2,1)} %wout_hbm.1, bf16[384,8192]{1,0:T(8,128)(2,1)} %bitcast.8, ...), custom_call_target="tpu_custom_call" | custom-call | tf_op jit(solution)/shard_map/pallas_call | solution.py:491
  58.4 1.4 %copy.17 = bf16[16,1536]{1,0:T(8,128)(2,1)} copy(bf16[16,1536]{1,0:T(8,128)(2,1)} %shard_map.145) | data formatting | bytes 98304

commit v6 on v5

--- a/solution.py
+++ b/solution.py
@@ -18,6 +18,7 @@
 FAR = [oz * 4 + ox for oz, ox in reversed(ORDER) if (oz, ox) != (0, 0)]
 CHUNKS = [(0, 7), (7, 11), (11, 16)]
 DIRECT = 11
+SPLIT = 7
 X_FIRST = [(1, 2), (3, 2)]
 LOW = -1e30
 MESH = pl.DeviceIdType.MESH
@@ -52,7 +53,7 @@
     hid, wqkv, wout, kbuf, vbuf, up, down,
     pm_send, pm_recv, q_send, q_recv, q6, thr, part, part_send, part_recv, gather_t,
     rotated, value_new, proj, proj_recv, att, att_peer, wout_peer,
-    mask_send, mask_recv, slot_place, tok_send, tok, mixed, mixed_send, mixed_recv,
+    mask_send, mask_recv, slot_place, tok_send, tok, mixed_send, mixed_recv,
     local_sem, send_sem, recv_sem,
 ):
     me = lax.axis_index("req")
@@ -135,6 +136,17 @@
         return slot_copy(6, s, mask_send, mask_recv.at[pl.ds(16 * s, 16)], far_req(s))
 
     core = kv % 2
+    half = model // 2
+
+    def half_back(s, h):
+        lanes = pl.ds(half * h, half)
+        return slot_copy(
+            5 + 2 * h, s, mixed_send.at[pl.ds(16 * s, 16), lanes], mixed_recv.at[s, :, lanes],
+            near_req(s),
+        )
+
+    def back_copies(s):
+        return [half_back(s, 0), half_back(s, 1)] if s >= SPLIT else [back_copy(s)]
 
     def token_copy(s):
         oz, ox = ORDER[s]
@@ -280,7 +292,6 @@
     eye_16 = (iota((16, 16), 0) == iota((16, 16), 1)).astype(F32).astype(BF16)
     mask_send[...] = dot_nt(eye_16, chosen.astype(BF16)).astype(BF16)
     mask_recv[0:16, :] = mask_send[...]
-    each(1, n_req, lambda s: mask_copy(s).start())
     loads[7].start()
     loads[8].start()
     loads[6].wait()
@@ -290,6 +301,7 @@
     place_slot = (slot_col == iota((blocks, n_slot), 1).astype(F32)).astype(F32).astype(BF16)
     slot_place[...] = (iota((n_slot, blocks), 0).astype(F32) == slot_row).astype(F32).astype(BF16)
     wait_recv_all(*queries)
+    each(1, n_req, lambda s: mask_copy(s).start())
     arrived = dot_nn(place_slot, q_recv[...])
     zeros = jnp.zeros((blocks, HD), BF16)
     for q in range(3):
@@ -394,17 +406,29 @@
     swap.start()
 
     own_rows = att[:, pl.ds(core, 1)].reshape(64, 256)[:, :192]
-    own_part = [dot_nn(own_rows, wout[:, n : n + 512]) for n in range(0, model, 512)]
+    def sum_copy(h, o):
+        peer = (kv + 2 * o) % n_kv
+        lanes = pl.ds(half * h, half)
+        return pltpu.make_async_remote_copy(
+            src_ref=proj.at[peer // 2, :, lanes], dst_ref=proj_recv.at[o, :, lanes],
+            send_sem=send_sem.at[3, 4 * h + o], recv_sem=recv_sem.at[3, 4 * h + o],
+            device_id={"kv": peer}, device_id_type=MESH,
+        )
+
+    own_part = [dot_nn(own_rows, wout[:, n : n + half]) for n in range(0, model, half)]
     share_w.wait_recv()
     swap.wait_recv()
     peer_rows = att_peer[...].reshape(64, 256)[:, :192]
-    for n in range(0, model, 512):
-        part_n = own_part[n // 512] + dot_nn(peer_rows, wout_peer[:, n : n + 512])
-        proj[:, :, n : n + 512] = part_n.astype(BF16).reshape(4, 16, 512)
-    sums = (3, 4, "y", lambda peer: proj.at[peer // 2], proj_recv)
-    start_all(*sums)
+    for h in range(2):
+        lanes = pl.ds(half * h, half)
+        both = own_part[h] + dot_nn(peer_rows, wout_peer[:, lanes])
+        proj[:, :, lanes] = both.astype(BF16).reshape(4, 16, half)
+        for o in (2, 1, 3):
+            sum_copy(h, o).start()
     own_proj = proj[pl.ds(kv // 2, 1)].reshape(16, model).astype(F32)
-    wait_recv_all(*sums)
+    for h in range(2):
+        for o in range(1, 4):
+            sum_copy(h, o).wait_recv()
     after_attn = hid[token_rows(kv), :].astype(F32)
     total = own_proj
     for k in range(1, 4):
@@ -432,35 +456,43 @@
         logits = jnp.where(mask_recv[here, :].astype(F32) > 0.0, logits, LOW)
         gates = jnp.exp(logits - jnp.max(logits, 1, keepdims=True))
         gates = gates / jnp.sum(gates, 1, keepdims=True)
+        acts, gains = [], []
         for e in range(2):
-            weight = jnp.sum(jnp.where(gate_lane == 2 * me + e, gates, 0.0), 1, keepdims=True)
-            acts = []
+            gains.append(jnp.sum(jnp.where(gate_lane == 2 * me + e, gates, 0.0), 1, keepdims=True))
+            these = []
             for f in range(0, FFE, 256):
                 gate = dot_nn(inputs, up[e, :, f : f + 256])
                 lift = dot_nn(inputs, up[e, :, FFE + f : FFE + f + 256])
-                acts.append((gate * jax.nn.sigmoid(gate) * lift).astype(BF16))
-            act = jnp.concatenate(acts, 1)
-            for n in range(0, model, 256):
-                made = dot_nn(act, down[e, :, n : n + 256]).astype(BF16).astype(F32) * weight
-                if e == 0:
-                    mixed[0:count, n : n + 256] = made
-                else:
-                    made = mixed[0:count, n : n + 256] + made
-                    mixed_send[here, n : n + 256] = made.astype(BF16)
-        each(max(first, 1), last, lambda s: back_copy(s).start())
-
+                these.append((gate * jax.nn.sigmoid(gate) * lift).astype(BF16))
+            acts.append(jnp.concatenate(these, 1))
+        for h in range(2):
+            for n in range(half * h, half * (h + 1), 256):
+                made = [
+                    dot_nn(acts[e], down[e, :, n : n + 256]).astype(BF16).astype(F32) * gains[e]
+                    for e in range(2)
+                ]
+                mixed_send[here, n : n + 256] = (made[0] + made[1]).astype(BF16)
+            if first < SPLIT and h == 1:
+                each(max(first, 1), last, lambda s: back_copy(s).start())
+            elif first >= SPLIT:
+                each(first, last, lambda s: half_back(s, h).start())
+
+    each(1, n_req, lambda s: mask_copy(s).wait_send())
+    each(1, n_req, lambda s: token_copy(s).wait_send())
+    each(1, n_req, lambda s: [copy.wait_send() for copy in back_copies(s)])
+    share_w.wait_send()
+    swap.wait_send()
+    for h in range(2):
+        for o in range(1, 4):
+            sum_copy(h, o).wait_send()
+    for exchange in (presence, queries, partials):
+        wait_send_all(*exchange)
     result = mixed_send[0:16, :].astype(F32)
     for d in range(1, n_req):
-        back_copy(d).wait_recv()
+        for copy in back_copies(d):
+            copy.wait_recv()
         result = result + mixed_recv[d].astype(F32)
     out_ref[...] = (after_attn + result).astype(BF16)
-    each(1, n_req, lambda s: mask_copy(s).wait_send())
-    each(1, n_req, lambda s: token_copy(s).wait_send())
-    each(1, n_req, lambda s: back_copy(s).wait_send())
-    share_w.wait_send()
-    swap.wait_send()
-    for exchange in (presence, queries, partials, sums):
-        wait_send_all(*exchange)
 
 
 def shards(
@@ -486,7 +518,7 @@
         ((4, 2, 16, 256), BF16), ((4, 16, 256), BF16), ((192, model), BF16),
         ((16, 128), BF16), ((256, 128), BF16), ((n_slot, blocks), BF16),
         ((16, model), BF16), ((256, model), BF16),
-        ((112, model), F32), ((256, model), BF16), ((16, 16, model), BF16),
+        ((256, model), BF16), ((16, 16, model), BF16),
     ]
     return pl.pallas_call(
         kernel,
@@ -501,8 +533,8 @@
         + [pltpu.VMEM(shape, dtype) for shape, dtype in scratch]
         + [
             pltpu.SemaphoreType.DMA((15,)),
-            pltpu.SemaphoreType.DMA((7, 16)),
-            pltpu.SemaphoreType.DMA((7, 16)),
+            pltpu.SemaphoreType.DMA((8, 16)),
+            pltpu.SemaphoreType.DMA((8, 16)),
         ],
         compiler_params=pltpu.CompilerParams(
             collective_id=0, has_side_effects=True, vmem_limit_bytes=56 << 20

time: 60 us -> 58.9 us (0.982)
  Pallas kernels: 58.4 us -> 57.3 us
    pallas_call x1, Pallas kernels: 58.4 us -> 57.3 us  [shards(): pl.pallas_call(kernel, out_shape=jax.ShapeDtypeStruct((16, model), BF16),...]
where the time goes in v6:
time: 58.9 us; the launch traced here: 58.7 us
  Pallas kernels  57.3 us (97%)
  local copies, waits for them, and re-layouts  1.42 us (2%)
    pallas_call x1, Pallas kernels, shards(): pl.pallas_call(kernel, out_shape=jax.ShapeDtypeStruct((16, model), BF16),...  57.3 us
    unnamed x1, local copies, waits for them, and re-layouts  1.42 us

profile of v6, /device:TPU:0, one launch (start us, length us, event | category | flops | bytes accessed | tf_op | source)
XLA Modules:
  0.0 58.7 jit_solution(3350660840134118371)
XLA Ops:
  0.0 57.3 %shard_map.145 = bf16[16,1536]{1,0:T(8,128)(2,1)} custom-call(bf16[128,1536]{1,0:T(8,128)(2,1)} %hidden_hbm.1, f32[12,128]{1,0:T(8,128)} %bitcast.11, bf16[192,1536]{1,0:T(8,128)(2,1)} %wq_hbm.1, bf16[64,1536]{1,0:T(8,128)(2,1)} %wk_hbm.1, bf16[64,1536]{1,0:T(8,128)(2,1)} %wv_hbm.1, bf16[192,1536]{1,0:T(8,128)(2,1)} %wout_hbm.1, bf16[384,8192]{1,0:T(8,128)(2,1)} %bitcast.8, ...), custom_call_target="tpu_custom_call" | custom-call | tf_op jit(solution)/shard_map/pallas_call | solution.py:523
  57.3 1.4 %copy.17 = bf16[16,1536]{1,0:T(8,128)(2,1)} copy(bf16[16,1536]{1,0:T(8,128)(2,1)} %shard_map.145) | data formatting | bytes 98304
